TPU v7x, 32 devices: a whole 2x2x4 slice. The times are simulated.
32 devices in a mesh: grp: 8 (over z, y), tp: 2 (over x), sp: 2 (over core).
Axes of the slice: x: 2, y: 2, z: 4, core: 2. Of those that a mesh axis runs over, the one named last changes fastest.
Arguments:
- tokens: bfloat16 [12288, 1536], P(('grp', 'sp')), may hold values from -6 to 6
- text_states: bfloat16 [2048, 4096], P(('grp', 'sp')), may hold values from -6 to 6
- condition: bfloat16 [8, 1024], P('grp'), may hold values from -6 to 6
- positions: int32 [3, 12288], P(None, ('grp', 'sp')), may hold values from 0 to 16, as said below
- counts: int32 [8], replicated, may hold values from 84 to 1536, as said below
- cotangent: bfloat16 [12288, 1536], P(('grp', 'sp')), may hold values from -6 to 6
- w_mod: bfloat16 [1024, 6144], P('sp', 'tp'), may hold values from -0.1875 to 0.1875
- norm_gains: float32 [4, 1536], replicated, may hold values from 0.1 to 1.9
- qk_gains: float32 [2, 1536], P(None, 'tp'), may hold values from 0.1 to 1.9
- cross_gate: float32 [24], P('tp'), may hold values from 0.25 to 1
- w_query: bfloat16 [1536, 1536], P('sp', 'tp'), may hold values from -0.15625 to 0.15625
- w_key: bfloat16 [1536, 1536], P('sp', 'tp'), may hold values from -0.15625 to 0.15625
- w_value: bfloat16 [1536, 1536], P('sp', 'tp'), may hold values from -0.15625 to 0.15625
- w_out: bfloat16 [1536, 1536], P('tp', 'sp'), may hold values from -0.15625 to 0.15625
- w_cross_query: bfloat16 [1536, 1536], P('sp', 'tp'), may hold values from -0.15625 to 0.15625
- w_cross_key: bfloat16 [4096, 1536], P('sp', 'tp'), may hold values from -0.09375 to 0.09375
- w_cross_value: bfloat16 [4096, 1536], P('sp', 'tp'), may hold values from -0.09375 to 0.09375
- w_gate: bfloat16 [1536, 4096], P('sp', 'tp'), may hold values from -0.15625 to 0.15625
- w_up: bfloat16 [1536, 4096], P('sp', 'tp'), may hold values from -0.15625 to 0.15625
- w_down: bfloat16 [4096, 1536], P('tp', 'sp'), may hold values from -0.09375 to 0.09375
Outputs:
- output: bfloat16 [12288, 1536], P(('grp', 'sp'))
- grad_tokens: float32 [12288, 1536], P(('grp', 'sp'))
- grad_text: float32 [2048, 4096], P(('grp', 'sp'), 'tp')
- grad_w_mod: float32 [1024, 6144], P(('grp', 'sp'), 'tp')
- grad_norm_gains: float32 [4, 1536], replicated
- grad_qk_gains: float32 [2, 1536], P(None, 'tp')
- grad_cross_gate: float32 [24], P('tp')
- grad_w_query: float32 [1536, 1536], P(('grp', 'sp'), 'tp')
- grad_w_key: float32 [1536, 1536], P(('grp', 'sp'), 'tp')
- grad_w_value: float32 [1536, 1536], P(('grp', 'sp'), 'tp')
- grad_w_out: float32 [1536, 1536], P('tp', ('grp', 'sp'))
- grad_w_cross_query: float32 [1536, 1536], P(('grp', 'sp'), 'tp')
- grad_w_cross_key: float32 [4096, 1536], P(('grp', 'sp'), 'tp')
- grad_w_cross_value: float32 [4096, 1536], P(('grp', 'sp'), 'tp')
- grad_w_gate: float32 [1536, 4096], P(('grp', 'sp'), 'tp')
- grad_w_up: float32 [1536, 4096], P(('grp', 'sp'), 'tp')
- grad_w_down: float32 [4096, 1536], P('tp', ('grp', 'sp'))
Inputs may be any that keep to these rules, and one draw needn't show every extreme that they name: `counts`: valid tokens of each clip, at most 1536; at least one clip fills all 1536 slots. `positions`: for each clip, row 0 holds the frame, row 1 the row and row 2 the column of each valid slot: each frame is some rows of a fixed width plus one nextline column, followed by one nextframe token with the row past the last and column 0; padding slots hold zeros.
All inputs are finite; a program needn't handle non-finite values.
Results may differ from a plain program's by a relative error of at most 0.02.
Values may be sent and summed in bfloat16 or wider, within the bound.
No kernel may reach another device: no remote copies, remote signals or barrier semaphores. Data moves between devices by JAX's collectives and lax.ppermute only.
A program may use at most 448 MiB of HBM per device.

v0:
```python
import jax
import jax.numpy as jnp
from jax import lax
from jax.sharding import PartitionSpec as P

HEAD_DIM = 64


EPSILON = 1e-05
ROPE_BASE = 10000.0


def rms_parts(values):
    factor = lax.rsqrt(jnp.mean(values * values, axis=-1, keepdims=True) + EPSILON)
    return (values * factor, factor)


def rms_back(gradient, normed, factor):
    return factor * (gradient - normed * jnp.mean(gradient * normed, axis=-1, keepdims=True))


def rope_angles(positions):
    pieces = []
    for axis_no, span_dims in ((0, 16), (1, 24), (2, 24)):
        frequency = ROPE_BASE ** (-2.0 * jnp.arange(span_dims // 2, dtype=jnp.float32) / span_dims)
        pieces.append(positions[axis_no].astype(jnp.float32)[:, None] * frequency[None, :])
    return jnp.concatenate(pieces, axis=1)


def rotate(values, cosine_table, sine_table):
    half_dims = values.shape[-1] // 2
    first_half = values[..., :half_dims]
    second_half = values[..., half_dims:]
    return jnp.concatenate(
        [
            first_half * cosine_table - second_half * sine_table,
            first_half * sine_table + second_half * cosine_table,
        ],
        axis=-1,
    )


def log_sum_exp(scores):
    top_score = jnp.max(scores, axis=-1, keepdims=True)
    return top_score + jnp.log(jnp.sum(jnp.exp(scores - top_score), axis=-1, keepdims=True))


def tp_sum(partial_sum):
    return lax.psum(partial_sum.astype(jnp.bfloat16), "tp").astype(jnp.float32)


def pair_plan(
    tokens,
    text_states,
    condition,
    positions,
    counts,
    cotangent,
    w_mod,
    norm_gains,
    qk_gains,
    cross_gate,
    w_query,
    w_key,
    w_value,
    w_out,
    w_cross_query,
    w_cross_key,
    w_cross_value,
    w_gate,
    w_up,
    w_down,
):
    gathered = (
        lax.all_gather(w_query, "sp", axis=0, tiled=True),
        lax.all_gather(w_key, "sp", axis=0, tiled=True),
        lax.all_gather(w_value, "sp", axis=0, tiled=True),
        lax.all_gather(w_cross_query, "sp", axis=0, tiled=True),
        lax.all_gather(w_cross_key, "sp", axis=0, tiled=True),
        lax.all_gather(w_cross_value, "sp", axis=0, tiled=True),
        lax.all_gather(w_gate, "sp", axis=0, tiled=True),
        lax.all_gather(w_up, "sp", axis=0, tiled=True),
        lax.all_gather(w_mod, "sp", axis=0, tiled=True),
        lax.all_gather(w_out, "sp", axis=1, tiled=True),
        lax.all_gather(w_down, "sp", axis=1, tiled=True),
    )
    (
        w_query,
        w_key,
        w_value,
        w_cross_query,
        w_cross_key,
        w_cross_value,
        w_gate,
        w_up,
        w_mod,
        w_out,
        w_down,
    ) = gathered
    rows_here = tokens.shape[0]
    model_width = tokens.shape[1]
    local_width = w_query.shape[1]
    heads_here = local_width // HEAD_DIM
    text_rows = text_states.shape[0]
    sequence_len = rows_here * lax.axis_size("sp")
    scaling = HEAD_DIM ** (-0.5)
    group_no = lax.axis_index("grp")
    valid_count = jnp.sum(jnp.where(jnp.arange(counts.shape[0]) == group_no, counts, 0))
    group_share = valid_count.astype(jnp.float32) / jnp.sum(counts).astype(jnp.float32)
    row_ids = lax.axis_index("sp") * rows_here + jnp.arange(rows_here)
    valid_rows = (row_ids < valid_count).astype(jnp.float32)[:, None]
    key_live = (jnp.arange(sequence_len) < valid_count)[None, None, :]
    part_mod = jnp.dot(condition, w_mod, preferred_element_type=jnp.float32)
    modulation = lax.all_gather(part_mod, "tp", axis=1, tiled=True)[0]
    scale_attn = modulation[:model_width]
    gate_attn = modulation[model_width : 2 * model_width]
    scale_ffn = modulation[2 * model_width : 3 * model_width]
    gate_ffn = modulation[3 * model_width :]
    tokens_wide = tokens.astype(jnp.float32)
    normed_one, factor_one = rms_parts(tokens_wide)
    lift_attn = norm_gains[0] * (1.0 + scale_attn)
    normed_in = (normed_one * lift_attn).astype(jnp.bfloat16)
    query_pre = jnp.dot(normed_in, w_query, preferred_element_type=jnp.float32).reshape(
        rows_here, heads_here, HEAD_DIM
    )
    key_pre = jnp.dot(normed_in, w_key, preferred_element_type=jnp.float32).reshape(
        rows_here, heads_here, HEAD_DIM
    )
    value_low = jnp.dot(normed_in, w_value, preferred_element_type=jnp.float32).astype(jnp.bfloat16)
    query_gain = qk_gains[0].reshape(heads_here, HEAD_DIM)
    key_gain = qk_gains[1].reshape(heads_here, HEAD_DIM)
    query_norm, query_factor = rms_parts(query_pre)
    key_norm, key_factor = rms_parts(key_pre)
    angles = rope_angles(positions)
    cosine_table = jnp.cos(angles)[:, None, :]
    sine_table = jnp.sin(angles)[:, None, :]
    query_rot = rotate(query_norm * query_gain, cosine_table, sine_table).astype(jnp.bfloat16)
    key_rot = rotate(key_norm * key_gain, cosine_table, sine_table).astype(jnp.bfloat16)
    key_all, value_all = (
        lax.all_gather(key_rot.reshape(rows_here, local_width), "sp", axis=0, tiled=True),
        lax.all_gather(value_low, "sp", axis=0, tiled=True),
    )
    key_all = key_all.reshape(sequence_len, heads_here, HEAD_DIM)
    value_all = value_all.reshape(sequence_len, heads_here, HEAD_DIM)

    def self_scores():
        raw_scores = (
            jnp.einsum("qhd,khd->hqk", query_rot, key_all, preferred_element_type=jnp.float32)
            * scaling
        )
        return jnp.where(key_live, raw_scores, -1e30)

    scores = self_scores()
    self_lse = log_sum_exp(scores)
    self_probs = jnp.exp(scores - self_lse).astype(jnp.bfloat16)
    self_mix = jnp.einsum("hqk,khd->qhd", self_probs, value_all, preferred_element_type=jnp.float32)
    cross_query = (
        jnp.dot(normed_in, w_cross_query, preferred_element_type=jnp.float32)
        .astype(jnp.bfloat16)
        .reshape(rows_here, heads_here, HEAD_DIM)
    )
    cross_key_low = jnp.dot(text_states, w_cross_key, preferred_element_type=jnp.float32).astype(
        jnp.bfloat16
    )
    cross_value_low = jnp.dot(
        text_states, w_cross_value, preferred_element_type=jnp.float32
    ).astype(jnp.bfloat16)
    cross_keys, cross_values = (
        lax.all_gather(cross_key_low, "sp", axis=0, tiled=True),
        lax.all_gather(cross_value_low, "sp", axis=0, tiled=True),
    )
    text_len = cross_keys.shape[0]
    cross_keys = cross_keys.reshape(text_len, heads_here, HEAD_DIM)
    cross_values = cross_values.reshape(text_len, heads_here, HEAD_DIM)

    def cross_scores_of():
        return (
            jnp.einsum("qhd,khd->hqk", cross_query, cross_keys, preferred_element_type=jnp.float32)
            * scaling
        )

    cross_scores = cross_scores_of()
    cross_lse = log_sum_exp(cross_scores)
    cross_probs = jnp.exp(cross_scores - cross_lse).astype(jnp.bfloat16)
    cross_mix = jnp.einsum(
        "hqk,khd->qhd", cross_probs, cross_values, preferred_element_type=jnp.float32
    )
    gate_tanh = jnp.tanh(cross_gate)[None, :, None]
    mixed_heads = (
        (self_mix + gate_tanh * cross_mix).reshape(rows_here, local_width).astype(jnp.bfloat16)
    )
    attended = tp_sum(jnp.dot(mixed_heads, w_out, preferred_element_type=jnp.float32))
    attn_norm, attn_factor = rms_parts(attended)
    tanh_attn = jnp.tanh(gate_attn)
    middle = tokens_wide + tanh_attn * attn_norm * norm_gains[1]
    normed_two, factor_two = rms_parts(middle)
    lift_ffn = norm_gains[2] * (1.0 + scale_ffn)
    normed_mid = (normed_two * lift_ffn).astype(jnp.bfloat16)
    gate_pre = jnp.dot(normed_mid, w_gate, preferred_element_type=jnp.float32)
    up_pre = jnp.dot(normed_mid, w_up, preferred_element_type=jnp.float32)
    sigmoid_gate = jax.nn.sigmoid(gate_pre)
    silu_gate = gate_pre * sigmoid_gate
    hidden = (silu_gate * up_pre).astype(jnp.bfloat16)
    reduced = tp_sum(jnp.dot(hidden, w_down, preferred_element_type=jnp.float32))
    down_norm, down_factor = rms_parts(reduced)
    tanh_ffn = jnp.tanh(gate_ffn)
    output = (middle + tanh_ffn * down_norm * norm_gains[3]).astype(jnp.bfloat16)
    grad_out = cotangent.astype(jnp.float32) * valid_rows
    grad_gate_ffn = jnp.sum(grad_out * down_norm * norm_gains[3], axis=0) * (
        1.0 - tanh_ffn * tanh_ffn
    )
    grad_gain_four = jnp.sum(grad_out * tanh_ffn * down_norm, axis=0)
    grad_reduced = rms_back(grad_out * tanh_ffn * norm_gains[3], down_norm, down_factor).astype(
        jnp.bfloat16
    )
    grad_w_down = group_share * jnp.einsum(
        "tf,td->fd", hidden, grad_reduced, preferred_element_type=jnp.float32
    )
    grad_hidden = jnp.einsum("td,fd->tf", grad_reduced, w_down, preferred_element_type=jnp.float32)
    grad_up = (grad_hidden * silu_gate).astype(jnp.bfloat16)
    grad_gate_pre = (
        grad_hidden * up_pre * sigmoid_gate * (1.0 + gate_pre * (1.0 - sigmoid_gate))
    ).astype(jnp.bfloat16)
    grad_w_gate = group_share * jnp.einsum(
        "tc,tf->cf", normed_mid, grad_gate_pre, preferred_element_type=jnp.float32
    )
    grad_w_up = group_share * jnp.einsum(
        "tc,tf->cf", normed_mid, grad_up, preferred_element_type=jnp.float32
    )
    grad_normed_mid = tp_sum(
        jnp.einsum("tf,cf->tc", grad_gate_pre, w_gate, preferred_element_type=jnp.float32)
        + jnp.einsum("tf,cf->tc", grad_up, w_up, preferred_element_type=jnp.float32)
    )
    grad_gain_three = jnp.sum(grad_normed_mid * normed_two * (1.0 + scale_ffn), axis=0)
    grad_scale_ffn = jnp.sum(grad_normed_mid * normed_two * norm_gains[2], axis=0)
    grad_middle = grad_out + rms_back(grad_normed_mid * lift_ffn, normed_two, factor_two)
    grad_gate_attn = jnp.sum(grad_middle * attn_norm * norm_gains[1], axis=0) * (
        1.0 - tanh_attn * tanh_attn
    )
    grad_gain_two = jnp.sum(grad_middle * tanh_attn * attn_norm, axis=0)
    grad_attended = rms_back(
        grad_middle * tanh_attn * norm_gains[1], attn_norm, attn_factor
    ).astype(jnp.bfloat16)
    grad_w_out = group_share * jnp.einsum(
        "th,td->hd", mixed_heads, grad_attended, preferred_element_type=jnp.float32
    )
    grad_mixed = (
        jnp.einsum("td,hd->th", grad_attended, w_out, preferred_element_type=jnp.float32)
        .astype(jnp.bfloat16)
        .reshape(rows_here, heads_here, HEAD_DIM)
    )
    grad_mixed_wide = grad_mixed.astype(jnp.float32)
    tanh_cross = jnp.tanh(cross_gate)
    grad_cross_gate = jnp.sum(grad_mixed_wide * cross_mix, axis=(0, 2)) * (
        1.0 - tanh_cross * tanh_cross
    )
    grad_cross_mix = (gate_tanh * grad_mixed_wide).astype(jnp.bfloat16)
    scores = self_scores()
    probs_wide = jnp.exp(scores - self_lse)
    probs_low = probs_wide.astype(jnp.bfloat16)
    grad_probs = jnp.einsum(
        "qhd,khd->hqk", grad_mixed, value_all, preferred_element_type=jnp.float32
    )
    grad_scores = (
        probs_wide * (grad_probs - jnp.sum(probs_wide * grad_probs, axis=-1, keepdims=True))
    ).astype(jnp.bfloat16)
    grad_query_rot = (
        jnp.einsum("hqk,khd->qhd", grad_scores, key_all, preferred_element_type=jnp.float32)
        * scaling
    )
    score_rows = grad_scores
    prob_rows = probs_low
    grad_key_rows = (
        jnp.einsum("hqk,qhd->khd", score_rows, query_rot, preferred_element_type=jnp.float32)
        * scaling
    )
    grad_value_rows = jnp.einsum(
        "hqk,qhd->khd", prob_rows, grad_mixed, preferred_element_type=jnp.float32
    )
    key_grads = lax.psum_scatter(
        jnp.concatenate(
            [
                grad_key_rows.reshape(rows_here * lax.axis_size("sp"), local_width),
                grad_value_rows.reshape(rows_here * lax.axis_size("sp"), local_width),
            ],
            axis=1,
        ).astype(jnp.bfloat16),
        "sp",
        scatter_dimension=0,
        tiled=True,
    ).astype(jnp.float32)
    grad_key_rot = key_grads[:, :local_width].reshape(rows_here, heads_here, HEAD_DIM)
    grad_value = key_grads[:, local_width:].astype(jnp.bfloat16)
    grad_query_gained = rotate(grad_query_rot, cosine_table, -sine_table)
    grad_key_gained = rotate(grad_key_rot, cosine_table, -sine_table)
    grad_query_gain = jnp.sum(grad_query_gained * query_norm, axis=0)
    grad_key_gain = jnp.sum(grad_key_gained * key_norm, axis=0)
    grad_query = (
        rms_back(grad_query_gained * query_gain, query_norm, query_factor)
        .reshape(rows_here, local_width)
        .astype(jnp.bfloat16)
    )
    grad_key = (
        rms_back(grad_key_gained * key_gain, key_norm, key_factor)
        .reshape(rows_here, local_width)
        .astype(jnp.bfloat16)
    )
    cross_scores = cross_scores_of()
    cross_wide = jnp.exp(cross_scores - cross_lse)
    cross_low = cross_wide.astype(jnp.bfloat16)
    grad_cross_probs = jnp.einsum(
        "qhd,khd->hqk", grad_cross_mix, cross_values, preferred_element_type=jnp.float32
    )
    grad_cross_scores = (
        cross_wide
        * (grad_cross_probs - jnp.sum(cross_wide * grad_cross_probs, axis=-1, keepdims=True))
    ).astype(jnp.bfloat16)
    grad_cross_query = (
        (
            jnp.einsum(
                "hqk,khd->qhd", grad_cross_scores, cross_keys, preferred_element_type=jnp.float32
            )
            * scaling
        )
        .reshape(rows_here, local_width)
        .astype(jnp.bfloat16)
    )
    score_rows = grad_cross_scores
    prob_rows = cross_low
    grad_key_rows = (
        jnp.einsum("hqk,qhd->khd", score_rows, cross_query, preferred_element_type=jnp.float32)
        * scaling
    )
    grad_value_rows = jnp.einsum(
        "hqk,qhd->khd", prob_rows, grad_cross_mix, preferred_element_type=jnp.float32
    )
    text_grads_local = lax.psum_scatter(
        jnp.concatenate(
            [
                grad_key_rows.reshape(text_rows * lax.axis_size("sp"), local_width),
                grad_value_rows.reshape(text_rows * lax.axis_size("sp"), local_width),
            ],
            axis=1,
        ).astype(jnp.bfloat16),
        "sp",
        scatter_dimension=0,
        tiled=True,
    ).astype(jnp.float32)
    grad_cross_key = text_grads_local[:, :local_width].astype(jnp.bfloat16)
    grad_cross_value = text_grads_local[:, local_width:].astype(jnp.bfloat16)
    grad_w_cross_key = group_share * jnp.einsum(
        "tc,tf->cf", text_states, grad_cross_key, preferred_element_type=jnp.float32
    )
    grad_w_cross_value = group_share * jnp.einsum(
        "tc,tf->cf", text_states, grad_cross_value, preferred_element_type=jnp.float32
    )
    text_partial = jnp.einsum(
        "tf,cf->tc", grad_cross_key, w_cross_key, preferred_element_type=jnp.float32
    ) + jnp.einsum("tf,cf->tc", grad_cross_value, w_cross_value, preferred_element_type=jnp.float32)
    grad_text = lax.psum_scatter(
        text_partial.astype(jnp.bfloat16), "tp", scatter_dimension=1, tiled=True
    ).astype(jnp.float32)
    grad_w_query = group_share * jnp.einsum(
        "tc,tf->cf", normed_in, grad_query, preferred_element_type=jnp.float32
    )
    grad_w_key = group_share * jnp.einsum(
        "tc,tf->cf", normed_in, grad_key, preferred_element_type=jnp.float32
    )
    grad_w_value = group_share * jnp.einsum(
        "tc,tf->cf", normed_in, grad_value, preferred_element_type=jnp.float32
    )
    grad_w_cross_query = group_share * jnp.einsum(
        "tc,tf->cf", normed_in, grad_cross_query, preferred_element_type=jnp.float32
    )
    input_partial = jnp.einsum("tf,cf->tc", grad_query, w_query, preferred_element_type=jnp.float32)
    input_partial = input_partial + jnp.einsum(
        "tf,cf->tc", grad_key, w_key, preferred_element_type=jnp.float32
    )
    input_partial = input_partial + jnp.einsum(
        "tf,cf->tc", grad_value, w_value, preferred_element_type=jnp.float32
    )
    input_partial = input_partial + jnp.einsum(
        "tf,cf->tc", grad_cross_query, w_cross_query, preferred_element_type=jnp.float32
    )
    grad_normed_in = tp_sum(input_partial)
    grad_gain_one = jnp.sum(grad_normed_in * normed_one * (1.0 + scale_attn), axis=0)
    grad_scale_attn = jnp.sum(grad_normed_in * normed_one * norm_gains[0], axis=0)
    grad_tokens = grad_middle + rms_back(grad_normed_in * lift_attn, normed_one, factor_one)
    grad_modulation = jnp.concatenate(
        [grad_scale_attn, grad_gate_attn, grad_scale_ffn, grad_gate_ffn]
    )
    mod_width = w_mod.shape[1]
    own_modulation = lax.dynamic_slice_in_dim(
        grad_modulation, lax.axis_index("tp") * mod_width, mod_width
    )
    grad_w_mod = group_share * (
        condition.astype(jnp.float32).reshape(-1, 1) * own_modulation[None, :]
    )
    gain_grads = group_share * jnp.stack(
        [grad_gain_one, grad_gain_two, grad_gain_three, grad_gain_four]
    )
    qk_grads = group_share * jnp.stack([grad_query_gain.reshape(-1), grad_key_gain.reshape(-1)])
    small_sums = lax.psum((gain_grads, qk_grads, group_share * grad_cross_gate), ("grp", "sp"))
    reduced_all = (
        lax.psum_scatter(grad_w_mod, ("grp", "sp"), scatter_dimension=0, tiled=True),
        lax.psum_scatter(grad_w_query, ("grp", "sp"), scatter_dimension=0, tiled=True),
        lax.psum_scatter(grad_w_key, ("grp", "sp"), scatter_dimension=0, tiled=True),
        lax.psum_scatter(grad_w_value, ("grp", "sp"), scatter_dimension=0, tiled=True),
        lax.psum_scatter(grad_w_out, ("grp", "sp"), scatter_dimension=1, tiled=True),
        lax.psum_scatter(grad_w_cross_query, ("grp", "sp"), scatter_dimension=0, tiled=True),
        lax.psum_scatter(grad_w_cross_key, ("grp", "sp"), scatter_dimension=0, tiled=True),
        lax.psum_scatter(grad_w_cross_value, ("grp", "sp"), scatter_dimension=0, tiled=True),
        lax.psum_scatter(grad_w_gate, ("grp", "sp"), scatter_dimension=0, tiled=True),
        lax.psum_scatter(grad_w_up, ("grp", "sp"), scatter_dimension=0, tiled=True),
        lax.psum_scatter(grad_w_down, ("grp", "sp"), scatter_dimension=1, tiled=True),
    )
    return (
        output,
        grad_tokens,
        grad_text,
        reduced_all[0],
        small_sums[0],
        small_sums[1],
        small_sums[2],
        reduced_all[1],
        reduced_all[2],
        reduced_all[3],
        reduced_all[4],
        reduced_all[5],
        reduced_all[6],
        reduced_all[7],
        reduced_all[8],
        reduced_all[9],
        reduced_all[10],
    )


def on_device(
    tokens,
    text_states,
    condition,
    positions,
    counts,
    cotangent,
    w_mod,
    norm_gains,
    qk_gains,
    cross_gate,
    w_query,
    w_key,
    w_value,
    w_out,
    w_cross_query,
    w_cross_key,
    w_cross_value,
    w_gate,
    w_up,
    w_down,
):
    results = pair_plan(
        tokens,
        text_states,
        condition,
        positions,
        counts,
        cotangent,
        w_mod,
        norm_gains,
        qk_gains,
        cross_gate,
        w_query,
        w_key,
        w_value,
        w_out,
        w_cross_query,
        w_cross_key,
        w_cross_value,
        w_gate,
        w_up,
        w_down,
    )
    return results


def solution(mesh):
    placed = (
        P(("grp", "sp"), None),
        P(("grp", "sp"), None),
        P("grp", None),
        P(None, ("grp", "sp")),
        P(),
        P(("grp", "sp"), None),
        P("sp", "tp"),
        P(),
        P(None, "tp"),
        P("tp"),
        P("sp", "tp"),
        P("sp", "tp"),
        P("sp", "tp"),
        P("tp", "sp"),
        P("sp", "tp"),
        P("sp", "tp"),
        P("sp", "tp"),
        P("sp", "tp"),
        P("sp", "tp"),
        P("tp", "sp"),
    )
    return jax.shard_map(
        on_device,
        mesh=mesh,
        in_specs=placed,
        out_specs=(
            P(("grp", "sp"), None),
            P(("grp", "sp"), None),
            P(("grp", "sp"), "tp"),
            P(("grp", "sp"), "tp"),
            P(),
            P(None, "tp"),
            P("tp"),
            P(("grp", "sp"), "tp"),
            P(("grp", "sp"), "tp"),
            P(("grp", "sp"), "tp"),
            P("tp", ("grp", "sp")),
            P(("grp", "sp"), "tp"),
            P(("grp", "sp"), "tp"),
            P(("grp", "sp"), "tp"),
            P(("grp", "sp"), "tp"),
            P(("grp", "sp"), "tp"),
            P("tp", ("grp", "sp")),
        ),
        check_vma=False,
    )
```

profile of v0, /device:TPU:0, one launch (start us, length us, event | category | flops | bytes accessed | tf_op | source)
XLA Modules:
  0.0 2072.2 jit_solution(3635585133128280972)
XLA Ops:
  15.2 13.8 all-gather.15.cloned.1.call-done
  48.9 7.6 all-gather.23.cloned.1.call-done
  77.3 12.1 all-gather.27.cloned.1.call-done
  97.8 11.0 all-gather.31.cloned.1.call-done
  136.8 24.6 %fusion = (f32[12,768]{1,0:T(8,128)S(1)}, f32[12,768,1536]{2,1,0:T(8,128)}) fusion(pred[1536]{0:T(1024)(128)(4,1)S(1)} %iota_compare_fusion, bf16[1536,12,64]{0,2,1:T(8,128)(2,1)} %bitcast.164, bf16[768,12,32]{0,2,1:T(8,128)(2,1)} %get-tuple-element.119, bf16[768,12,32]{0,2,1:T(8,128)(2,1)} %get-tuple-element.118), kind=kOutput, calls=%fused_computation.5 | convolution fusion | flops 1856756736 | bytes 60200448 | tf_op jit(solution)/shard_map/qhd,khd->hqk/dot_general | solution.py:148
  161.4 18.9 exponential_reduce_fusion
  184.6 22.7 %fusion.61 = bf16[768,12,64]{0,2,1:T(8,128)(2,1)} fusion(f32[12,64,768]{2,1,0:T(8,128)} %fusion.70, bf16[1536,12,64]{0,2,1:T(8,128)(2,1)} %bitcast.167, f32[12]{0:T(128)S(1)} %copy-done.84, f32[12,768,1536]{2,1,0:T(8,128)} %get-tuple-element.136, f32[12,768]{1,0:T(8,128)S(1)} %log_add_fusion.1, pred[1536]{0:T(1024)(128)(4,1)S(1)} %iota_compare_fusion), kind=kOutput, calls=%fused_computation.126 | convolution fusion | flops 1870331904 | bytes 62559792 | tf_op jit(solution)/shard_map/hqk,khd->qhd/dot_general | solution.py:156
  214.9 67.9 %all-reduce.6.cloned.1.call-done = bf16[768,1536]{1,0:T(8,128)(2,1)} async-done(((bf16[768,1536]{1,0:T(8,128)(2,1)}), bf16[768,1536]{1,0:T(8,128)(2,1)}) %all-reduce.6.cloned.1.call-update) | async-done | bytes 2359312 | tf_op jit(solution)/shard_map/psum | solution.py:49
  291.0 9.9 all-gather.35.cloned.1.call-done
  301.0 9.5 fusion.118
  310.5 10.0 all-gather.37.cloned.1.call-done
  320.5 11.4 multiply_convert_fusion.4
  331.9 7.9 all-gather.39.cloned.1.call-done
  339.8 9.1 convolution_convert_fusion.1
  350.0 68.9 %all-reduce.8.cloned.1.call-done = bf16[768,1536]{1,0:T(8,128)(2,1)} async-done(((bf16[768,1536]{1,0:T(8,128)(2,1)}), bf16[768,1536]{1,0:T(8,128)(2,1)}) %all-reduce.8.cloned.1.call-update) | async-done | bytes 2359312 | tf_op jit(solution)/shard_map/psum | solution.py:49
  426.1 13.4 multiply_convert_fusion.2
  439.5 8.3 fusion.119
  447.8 9.4 add_convert_fusion.1
  457.4 68.6 %all-reduce.10.cloned.1.call-done = bf16[768,1536]{1,0:T(8,128)(2,1)} async-done(((bf16[768,1536]{1,0:T(8,128)(2,1)}), bf16[768,1536]{1,0:T(8,128)(2,1)}) %all-reduce.10.cloned.1.call-update) | async-done | bytes 2359312 | tf_op jit(solution)/shard_map/psum | solution.py:49
  526.1 6.2 multiply_reduce_fusion.3
  532.3 8.5 fusion.34
  546.2 23.6 %convolution_convert_fusion = bf16[12,64,1536]{2,1,0:T(8,128)(2,1)} fusion(bf16[768,12,64]{0,2,1:T(8,128)(2,1)S(1)} %bitcast.159, f32[12,768,1536]{2,1,0:T(8,128)} %get-tuple-element.136, f32[12,768]{1,0:T(8,128)S(1)} %log_add_fusion.1, pred[1536]{0:T(1024)(128)(4,1)S(1)} %iota_compare_fusion), kind=kOutput, calls=%fused_computation.103 | convolution fusion | flops 1869742080 | bytes 60200448 | tf_op jit(solution)/shard_map/hqk,qhd->khd/dot_general | solution.py:277
  569.8 40.7 %multiply_reduce_fusion = (f32[12,768]{1,0:T(8,128)S(1)}, f32[12,768,1536]{2,1,0:T(8,128)}) fusion(f32[12,768,1536]{2,1,0:T(8,128)} %get-tuple-element.136, f32[12,768]{1,0:T(8,128)S(1)} %log_add_fusion.1, pred[1536]{0:T(1024)(128)(4,1)S(1)} %iota_compare_fusion, bf16[768,12,64]{0,2,1:T(8,128)(2,1)S(1)} %bitcast.160, bf16[1536,12,64]{0,2,1:T(8,128)(2,1)} %bitcast.168), kind=kOutput, calls=%fused_computation.1 | convolution fusion | flops 1882708992 | bytes 116860416 | tf_op jit(solution)/shard_map/qhd,khd->hqk/dot_general | solution.py:261
  610.5 44.8 %multiply_convert_fusion = bf16[12,768,1536]{2,1,0:T(8,128)(2,1)} fusion(f32[12,768,1536]{2,1,0:T(8,128)} %get-tuple-element.140, f32[12,768,1536]{2,1,0:T(8,128)} %get-tuple-element.136, f32[12,768]{1,0:T(8,128)S(1)} %get-tuple-element.139, f32[12,768]{1,0:T(8,128)S(1)} %log_add_fusion.1, pred[1536]{0:T(1024)(128)(4,1)S(1)} %iota_compare_fusion), kind=kLoop, calls=%fused_computation | loop fusion | flops 84934656 | bytes 141633024 | tf_op jit(solution)/shard_map/convert_element_type | solution.py:266
  655.3 14.2 multiply_convert_fusion.5
  673.1 8.7 multiply_reduce_fusion.1
  681.8 11.2 multiply_convert_fusion.1
  710.2 15.2 multiply_bitcast_fusion.2
  750.4 6.3 fusion.21
  758.1 6.4 multiply_bitcast_fusion.1
  764.6 6.3 multiply_bitcast_fusion
  786.2 12.0 convolution_multiply_fusion
  798.2 10.1 convolution_multiply_fusion.2
  808.4 10.2 convolution_multiply_fusion.1
  840.9 6.4 multiply_multiply_fusion
  853.3 65.3 %all-reduce = (f32[4,1536]{1,0:T(4,128)}, f32[2,768]{1,0:T(2,128)}, f32[12]{0:T(128)}) all-reduce(f32[4,1536]{1,0:T(4,128)S(1)} %maximum_multiply_fusion, f32[2,768]{1,0:T(2,128)S(1)} %maximum_multiply_fusion.1, f32[12]{0:T(128)S(1)} %multiply_multiply_fusion.3), channel_id=1, replica_groups=mesh['grp'=8,'tp'=2,'sp'=2] {'grp','sp'}, use_global_device_ids=true, to_apply=%region_36.37 | all-reduce | flops 7692 | bytes 61536 | tf_op jit(solution)/shard_map/psum | solution.py:403
  918.6 6.7 fusion.23
  925.3 51.0 %reduce-scatter.33.cloned.1.call-done = f32[256,768]{0,1:T(8,128)} async-done(((f32[4096,768]{0,1:T(8,128)}), f32[256,768]{0,1:T(8,128)}) %reduce-scatter.33.cloned.1.call-update) | async-done | bytes 786448 | tf_op jit(solution)/shard_map/reduce_scatter | solution.py:411
  978.6 135.8 %reduce-scatter.35.cloned.1.call-done = f32[256,768]{0,1:T(8,128)} async-done(((f32[4096,768]{0,1:T(8,128)}), f32[256,768]{0,1:T(8,128)}) %reduce-scatter.35.cloned.1.call-update) | async-done | bytes 786448 | tf_op jit(solution)/shard_map/reduce_scatter | solution.py:412
  1116.7 77.0 %reduce-scatter.29.cloned.1.call-done = f32[768,96]{0,1:T(8,128)} async-done(((f32[768,1536]{0,1:T(8,128)}), f32[768,96]{0,1:T(8,128)}) %reduce-scatter.29.cloned.1.call-update) | async-done | bytes 294928 | tf_op jit(solution)/shard_map/reduce_scatter | solution.py:409
  1193.8 79.1 %reduce-scatter.31.cloned.1.call-done = f32[96,768]{1,0:T(8,128)} async-done(((f32[1536,768]{1,0:T(8,128)}), f32[96,768]{1,0:T(8,128)}) %reduce-scatter.31.cloned.1.call-update) | async-done | bytes 294928 | tf_op jit(solution)/shard_map/reduce_scatter | solution.py:410
  1272.8 138.8 %reduce-scatter.41.cloned.1.call-done = f32[2048,96]{0,1:T(8,128)} async-done(((f32[2048,1536]{0,1:T(8,128)}), f32[2048,96]{0,1:T(8,128)}) %reduce-scatter.41.cloned.1.call-update) | async-done | bytes 786448 | tf_op jit(solution)/shard_map/reduce_scatter | solution.py:415
  1411.6 138.7 %reduce-scatter.37.cloned.1.call-done = f32[96,2048]{1,0:T(8,128)} async-done(((f32[1536,2048]{1,0:T(8,128)}), f32[96,2048]{1,0:T(8,128)}) %reduce-scatter.37.cloned.1.call-update) | async-done | bytes 786448 | tf_op jit(solution)/shard_map/reduce_scatter | solution.py:413
  1550.3 138.6 %reduce-scatter.39.cloned.1.call-done = f32[96,2048]{1,0:T(8,128)} async-done(((f32[1536,2048]{1,0:T(8,128)}), f32[96,2048]{1,0:T(8,128)}) %reduce-scatter.39.cloned.1.call-update) | async-done | bytes 786448 | tf_op jit(solution)/shard_map/reduce_scatter | solution.py:414
  1688.9 79.3 %reduce-scatter.27.cloned.1.call-done = f32[96,768]{1,0:T(8,128)} async-done(((f32[1536,768]{1,0:T(8,128)}), f32[96,768]{1,0:T(8,128)}) %reduce-scatter.27.cloned.1.call-update) | async-done | bytes 294928 | tf_op jit(solution)/shard_map/reduce_scatter | solution.py:408
  1768.2 79.2 %reduce-scatter.23.cloned.1.call-done = f32[96,768]{1,0:T(8,128)} async-done(((f32[1536,768]{1,0:T(8,128)}), f32[96,768]{1,0:T(8,128)}) %reduce-scatter.23.cloned.1.call-update) | async-done | bytes 294928 | tf_op jit(solution)/shard_map/reduce_scatter | solution.py:406
  1847.4 79.0 %reduce-scatter.25.cloned.1.call-done = f32[96,768]{1,0:T(8,128)} async-done(((f32[1536,768]{1,0:T(8,128)}), f32[96,768]{1,0:T(8,128)}) %reduce-scatter.25.cloned.1.call-update) | async-done | bytes 294928 | tf_op jit(solution)/shard_map/reduce_scatter | solution.py:407
  1926.4 138.8 %reduce-scatter.21.cloned.1.call-done = f32[64,3072]{1,0:T(8,128)} async-done(((f32[1024,3072]{1,0:T(8,128)}), f32[64,3072]{1,0:T(8,128)}) %reduce-scatter.21.cloned.1.call-update) | async-done | bytes 786448 | tf_op jit(solution)/shard_map/reduce_scatter | solution.py:405
  (360 shorter events, 212.1 us)
Async XLA Ops:
  7.2 82.2 %copy-start = (bf16[128,4096]{1,0:T(8,128)(2,1)S(1)}, bf16[128,4096]{1,0:T(8,128)(2,1)}, u32[]{:S(2)}) copy-start(bf16[128,4096]{1,0:T(8,128)(2,1)} %param.21) | copy-start | bytes 3145732
  7.2 21.9 %all-gather.15.cloned.1.call-start = ((), (), s32[]{:S(2)}) async-start(), calls=%async_computation.14 | async-start | bytes 9437184 | tf_op jit(solution)/shard_map/all_gather | solution.py:83
  7.9 34.8 %all-gather.21.cloned.1.call-start = ((), (), s32[]{:S(2)}) async-start(), calls=%async_computation.17 | async-start | bytes 3538944 | tf_op jit(solution)/shard_map/all_gather | solution.py:75
  8.7 47.8 %all-gather.23.cloned.1.call-start = ((), (), s32[]{:S(2)}) async-start(), calls=%async_computation.18 | async-start | bytes 3538944 | tf_op jit(solution)/shard_map/all_gather | solution.py:76
  9.4 60.6 %all-gather.17.cloned.1.call-start = ((), (), s32[]{:S(2)}) async-start(), calls=%async_computation.15 | async-start | bytes 3538944 | tf_op jit(solution)/shard_map/all_gather | solution.py:77
  10.0 19.0 copy-start.78
  10.0 79.4 %all-gather.27.cloned.1.call-start = ((), (), s32[]{:S(2)}) async-start(), calls=%async_computation.20 | async-start | bytes 9437184 | tf_op jit(solution)/shard_map/all_gather | solution.py:80
  10.6 98.1 %all-gather.31.cloned.1.call-start = ((), (), s32[]{:S(2)}) async-start(), calls=%async_computation.22 | async-start | bytes 9437184 | tf_op jit(solution)/shard_map/all_gather | solution.py:79
  11.2 111.3 %all-gather.29.cloned.1.call-start = ((), (), s32[]{:S(2)}) async-start(), calls=%async_computation.21 | async-start | bytes 3538944 | tf_op jit(solution)/shard_map/all_gather | solution.py:78
  12.0 124.8 %all-gather.25.cloned.1.call-start = ((), (), s32[]{:S(2)}) async-start(), calls=%async_computation.19 | async-start | bytes 3538944 | tf_op jit(solution)/shard_map/all_gather | solution.py:140
  12.6 109.9 %copy-start.60 = (f32[768]{0:T(1024)}, f32[768]{0:T(1024)S(1)}, u32[]{:S(2)}) copy-start(f32[768]{0:T(1024)S(1)} %add_rsqrt_fusion.5) | copy-start | bytes 9220
  15.2 46.8 %copy-start.36 = (f32[768,32]{0,1:T(8,128)}, f32[768,32]{0,1:T(8,128)S(1)}, u32[]{:S(2)}) copy-start(f32[768,32]{0,1:T(8,128)S(1)} %get-tuple-element.130) | copy-start | bytes 294916
  38.9 83.6 %copy-start.46 = (f32[1536]{0:T(1024)}, f32[1536]{0:T(1024)S(1)}, u32[]{:S(2)}) copy-start(f32[1536]{0:T(1024)S(1)} %get-tuple-element.88) | copy-start | bytes 18436
  38.9 493.4 %copy-start.48 = (f32[1536]{0:T(1024)}, f32[1536]{0:T(1024)S(1)}, u32[]{:S(2)}) copy-start(f32[1536]{0:T(1024)S(1)} %get-tuple-element.86) | copy-start | bytes 18436
  65.0 115.3 %all-gather.19.cloned.1.call-start = ((), (), s32[]{:S(2)}) async-start(), calls=%async_computation.16 | async-start | bytes 3538944 | tf_op jit(solution)/shard_map/all_gather | solution.py:141
  74.8 132.5 %all-gather.33.cloned.1.call-start = ((), (), s32[]{:S(2)}) async-start(), calls=%async_computation.23 | async-start | bytes 3538944 | tf_op jit(solution)/shard_map/all_gather | solution.py:84
  75.4 207.4 %all-reduce.6.cloned.1.call-start = ((), (), s32[]{:S(2)}) async-start(), calls=%async_computation.24 | async-start | bytes 4718592 | tf_op jit(solution)/shard_map/psum | solution.py:49
  212.8 88.2 %all-gather.35.cloned.1.call-start = ((), (), s32[]{:S(2)}) async-start(), calls=%async_computation.25 | async-start | bytes 9437184 | tf_op jit(solution)/shard_map/all_gather | solution.py:81
  213.3 107.1 %all-gather.37.cloned.1.call-start = ((), (), s32[]{:S(2)}) async-start(), calls=%async_computation.26 | async-start | bytes 9437184 | tf_op jit(solution)/shard_map/all_gather | solution.py:82
  214.1 125.8 %all-gather.39.cloned.1.call-start = ((), (), s32[]{:S(2)}) async-start(), calls=%async_computation.27 | async-start | bytes 9437184 | tf_op jit(solution)/shard_map/all_gather | solution.py:85
  214.7 204.3 %all-reduce.8.cloned.1.call-start = ((), (), s32[]{:S(2)}) async-start(), calls=%async_computation.28 | async-start | bytes 4718592 | tf_op jit(solution)/shard_map/psum | solution.py:49
  348.9 72.4 %copy-start.50 = (f32[1536]{0:T(1024)S(1)}, f32[1536]{0:T(1024)}, u32[]{:S(2)}) copy-start(f32[1536]{0:T(1024)} %get-tuple-element.91) | copy-start | bytes 18436
  348.9 177.1 %all-reduce.10.cloned.1.call-start = ((), (), s32[]{:S(2)}) async-start(), calls=%async_computation.29 | async-start | bytes 4718592 | tf_op jit(solution)/shard_map/psum | solution.py:49
  350.0 182.3 %copy-start.62 = (f32[768]{0:T(1024)}, f32[768]{0:T(1024)S(1)}, u32[]{:S(2)}) copy-start(f32[768]{0:T(1024)S(1)} %fusion.87) | copy-start | bytes 9220
  421.3 111.0 %copy-start.64 = (f32[768]{0:T(1024)}, f32[768]{0:T(1024)S(1)}, u32[]{:S(2)}) copy-start(f32[768]{0:T(1024)S(1)} %add_rsqrt_fusion.2) | copy-start | bytes 9220
  426.1 13.4 copy-start.82
  447.8 78.3 %copy-start.70 = (f32[1536]{0:T(1024)S(1)}, f32[1536]{0:T(1024)}, u32[]{:S(2)}) copy-start(f32[1536]{0:T(1024)} %get-tuple-element.83) | copy-start | bytes 18436
  447.8 78.3 %copy-start.71 = (f32[1536]{0:T(1024)S(1)}, f32[1536]{0:T(1024)}, u32[]{:S(2)}) copy-start(f32[1536]{0:T(1024)} %get-tuple-element.89) | copy-start | bytes 18436
  457.2 268.5 %reduce-scatter.17.cloned.1.call-start = ((), (), s32[]{:S(2)}) async-start(), calls=%async_computation.30 | async-start | bytes 7077888 | tf_op jit(solution)/shard_map/reduce_scatter | solution.py:280
  546.2 150.6 %copy-start.14 = (bf16[768,768]{0,1:T(8,128)(2,1)}, bf16[768,768]{0,1:T(8,128)(2,1)S(1)}, u32[]{:S(2)}) copy-start(bf16[768,768]{0,1:T(8,128)(2,1)S(1)} %convolution_convert_fusion.3) | copy-start | bytes 3538948
  610.5 44.8 %copy-start.19 = (bf16[768,12,32]{0,2,1:T(8,128)(2,1)S(1)}, bf16[768,12,32]{0,2,1:T(8,128)(2,1)}, u32[]{:S(2)}) copy-start(bf16[768,12,32]{0,2,1:T(8,128)(2,1)} %get-tuple-element.118) | copy-start | bytes 1769476
  610.5 44.8 %copy-start.20 = (bf16[768,12,32]{0,2,1:T(8,128)(2,1)S(1)}, bf16[768,12,32]{0,2,1:T(8,128)(2,1)}, u32[]{:S(2)}) copy-start(bf16[768,12,32]{0,2,1:T(8,128)(2,1)} %get-tuple-element.119) | copy-start | bytes 1769476
  655.3 14.2 copy-start.30
  672.1 73.2 %reduce-scatter.43.cloned.1.call-start = ((), (), s32[]{:S(2)}) async-start(), calls=%async_computation.44 | async-start | bytes 1179648
  681.8 11.2 copy-start.23
  725.5 111.5 %all-reduce.12.cloned.1.call-start = ((), (), s32[]{:S(2)}) async-start(), calls=%async_computation.31 | async-start | bytes 4718592 | tf_op jit(solution)/shard_map/psum | solution.py:49
  745.1 106.0 %reduce-scatter.19.cloned.1.call-start = ((), (), s32[]{:S(2)}) async-start(), calls=%async_computation.32 | async-start | bytes 1572864 | tf_op jit(solution)/shard_map/reduce_scatter | solution.py:360
  756.8 219.5 %reduce-scatter.33.cloned.1.call-start = ((), (), s32[]{:S(2)}) async-start(), calls=%async_computation.39 | async-start | bytes 13369344 | tf_op jit(solution)/shard_map/reduce_scatter | solution.py:411
  764.5 349.9 %reduce-scatter.35.cloned.1.call-start = ((), (), s32[]{:S(2)}) async-start(), calls=%async_computation.40 | async-start | bytes 13369344 | tf_op jit(solution)/shard_map/reduce_scatter | solution.py:412
  770.9 422.9 %reduce-scatter.29.cloned.1.call-start = ((), (), s32[]{:S(2)}) async-start(), calls=%async_computation.37 | async-start | bytes 5013504 | tf_op jit(solution)/shard_map/reduce_scatter | solution.py:409
  778.1 494.7 %reduce-scatter.31.cloned.1.call-start = ((), (), s32[]{:S(2)}) async-start(), calls=%async_computation.38 | async-start | bytes 5013504 | tf_op jit(solution)/shard_map/reduce_scatter | solution.py:410
  785.5 626.1 %reduce-scatter.41.cloned.1.call-start = ((), (), s32[]{:S(2)}) async-start(), calls=%async_computation.43 | async-start | bytes 13369344 | tf_op jit(solution)/shard_map/reduce_scatter | solution.py:415
  798.2 752.1 %reduce-scatter.37.cloned.1.call-start = ((), (), s32[]{:S(2)}) async-start(), calls=%async_computation.41 | async-start | bytes 13369344 | tf_op jit(solution)/shard_map/reduce_scatter | solution.py:413
  808.3 880.6 %reduce-scatter.39.cloned.1.call-start = ((), (), s32[]{:S(2)}) async-start(), calls=%async_computation.42 | async-start | bytes 13369344 | tf_op jit(solution)/shard_map/reduce_scatter | solution.py:414
  818.6 949.6 %reduce-scatter.27.cloned.1.call-start = ((), (), s32[]{:S(2)}) async-start(), calls=%async_computation.36 | async-start | bytes 5013504 | tf_op jit(solution)/shard_map/reduce_scatter | solution.py:408
  824.4 1023.0 %reduce-scatter.23.cloned.1.call-start = ((), (), s32[]{:S(2)}) async-start(), calls=%async_computation.34 | async-start | bytes 5013504 | tf_op jit(solution)/shard_map/reduce_scatter | solution.py:406
  830.3 1096.1 %reduce-scatter.25.cloned.1.call-start = ((), (), s32[]{:S(2)}) async-start(), calls=%async_computation.35 | async-start | bytes 5013504 | tf_op jit(solution)/shard_map/reduce_scatter | solution.py:407
  836.3 1228.9 %reduce-scatter.21.cloned.1.call-start = ((), (), s32[]{:S(2)}) async-start(), calls=%async_computation.33 | async-start | bytes 13369344 | tf_op jit(solution)/shard_map/reduce_scatter | solution.py:405
  (77 other events, 214.5 us)
Sparse Core Ops, SparseCore 0:
  9.6 19.4 all-gather.14
  30.6 12.1 all-gather.20
  44.3 12.1 all-gather.22
  57.9 12.1 all-gather.16
  71.4 17.9 all-gather.26
  90.8 17.9 all-gather.30
  110.3 12.1 all-gather.28
  124.6 12.1 all-gather.24
  138.9 12.1 all-gather.18
  152.4 12.1 all-gather.32
  212.9 69.8 all-reduce.5
  284.2 16.7 all-gather.34
  302.5 17.9 all-gather.36
  321.9 17.9 all-gather.38
  349.1 69.8 all-reduce.7
  457.3 68.6 all-reduce.9
  672.3 12.3 reduce-scatter.16
  725.6 8.2 reduce-scatter.42
  745.2 68.8 all-reduce.11
  816.8 20.3 reduce-scatter.18
  841.3 135.0 reduce-scatter.32
  980.4 134.0 reduce-scatter.34
  1118.9 74.8 reduce-scatter.28
  1198.1 74.7 reduce-scatter.30
  1277.4 134.0 reduce-scatter.40
  1416.1 134.1 reduce-scatter.36
  1554.7 134.1 reduce-scatter.38
  1693.3 74.8 reduce-scatter.26
  1772.6 74.7 reduce-scatter.22
  1851.7 74.6 reduce-scatter.24
  1931.0 134.1 reduce-scatter.20
where the time goes:
time: 2080 us; the launch traced here: 2070 us
  waiting for transfers between devices  1440 us (69%)
  matrix products  359 us (17%)
  other arithmetic  147 us (7%)
  blocking collectives  74.6 us (4%)
  local copies, waits for them, and re-layouts  34.6 us (2%)
    psum x4, waiting for transfers between devices, tp_sum(): return lax.psum(partial_sum.astype(jnp.bfloat16), 'tp').astype(jnp.float32)  205 us
    reduce_scatter x1, waiting for transfers between devices, pair_plan(): lax.psum_scatter(grad_w_mod, ('grp', 'sp'), scatter_dimension=0, tiled=True)  139 us
    reduce_scatter x1, waiting for transfers between devices, pair_plan(): lax.psum_scatter(grad_w_down, ('grp', 'sp'), scatter_dimension=1, tiled=T...  139 us
    reduce_scatter x1, waiting for transfers between devices, pair_plan(): lax.psum_scatter(grad_w_gate, ('grp', 'sp'), scatter_dimension=0, tiled=T...  139 us
    reduce_scatter x1, waiting for transfers between devices, pair_plan(): lax.psum_scatter(grad_w_up, ('grp', 'sp'), scatter_dimension=0, tiled=True)  139 us
    reduce_scatter x1, waiting for transfers between devices, pair_plan(): lax.psum_scatter(grad_w_cross_value, ('grp', 'sp'), scatter_dimension=0,...  136 us
    reduce_scatter x1, waiting for transfers between devices, pair_plan(): lax.psum_scatter(grad_w_value, ('grp', 'sp'), scatter_dimension=0, tiled=...  79.3 us
    reduce_scatter x1, waiting for transfers between devices, pair_plan(): lax.psum_scatter(grad_w_query, ('grp', 'sp'), scatter_dimension=0, tiled=...  79.2 us
  transfers between devices with their start and end apart: 31, of which 25 were waited for; matrix products, arithmetic and copies ran while one was open for 16% of the time, Pallas kernels for 0%

commit v1 on v0

--- a/solution.py
+++ b/solution.py
@@ -45,8 +45,51 @@
     return top_score + jnp.log(jnp.sum(jnp.exp(scores - top_score), axis=-1, keepdims=True))
 
 
+def swap_sp(value):
+    size = lax.axis_size("sp")
+    return lax.ppermute(value, "sp", [(i, i ^ 1) for i in range(size)])
+
+
+def swap_tp(value):
+    size = lax.axis_size("tp")
+    return lax.ppermute(value, "tp", [(i, i ^ 1) for i in range(size)])
+
+
 def tp_sum(partial_sum):
-    return lax.psum(partial_sum.astype(jnp.bfloat16), "tp").astype(jnp.float32)
+    low = partial_sum.astype(jnp.bfloat16)
+    return low.astype(jnp.float32) + swap_tp(low).astype(jnp.float32)
+
+
+def turn_halves(values):
+    half = values.shape[-1] // 2
+    turned = jnp.concatenate([values[..., half:], values[..., :half]], axis=-1)
+    return jnp.where(lax.axis_index("sp") == 0, values, turned)
+
+
+def halve(values, axis, bit, send):
+    keep_part = lax.dynamic_index_in_dim(values, bit, axis, keepdims=False)
+    sent_part = lax.dynamic_index_in_dim(values, 1 - bit, axis, keepdims=False)
+    return keep_part.astype(jnp.float32) + send(sent_part).astype(jnp.float32)
+
+
+def weight_sum(partial_sum):
+    groups = lax.axis_size("grp")
+    bits = groups.bit_length() - 1
+    rows = partial_sum.shape[0] // (2 * groups)
+    width = partial_sum.shape[1]
+    values = partial_sum.astype(jnp.bfloat16).reshape((2,) * bits + (2, rows, width))
+    group_no = lax.axis_index("grp")
+    summed = halve(values, bits, lax.axis_index("sp"), swap_sp)
+    left = list(range(bits - 1, -1, -1))
+    for exponent in [0] + list(range(bits - 1, 0, -1)):
+        pairs = [(i, i ^ (1 << exponent)) for i in range(groups)]
+        axis = left.index(exponent)
+        left.pop(axis)
+        bit = (group_no >> exponent) & 1
+        summed = halve(
+            summed.astype(jnp.bfloat16), axis, bit, lambda sent: lax.ppermute(sent, "grp", pairs)
+        )
+    return summed
 
 
 def pair_plan(
@@ -71,35 +114,19 @@
     w_up,
     w_down,
 ):
-    gathered = (
-        lax.all_gather(w_query, "sp", axis=0, tiled=True),
-        lax.all_gather(w_key, "sp", axis=0, tiled=True),
-        lax.all_gather(w_value, "sp", axis=0, tiled=True),
-        lax.all_gather(w_cross_query, "sp", axis=0, tiled=True),
-        lax.all_gather(w_cross_key, "sp", axis=0, tiled=True),
-        lax.all_gather(w_cross_value, "sp", axis=0, tiled=True),
-        lax.all_gather(w_gate, "sp", axis=0, tiled=True),
-        lax.all_gather(w_up, "sp", axis=0, tiled=True),
-        lax.all_gather(w_mod, "sp", axis=0, tiled=True),
-        lax.all_gather(w_out, "sp", axis=1, tiled=True),
-        lax.all_gather(w_down, "sp", axis=1, tiled=True),
-    )
-    (
-        w_query,
-        w_key,
-        w_value,
-        w_cross_query,
-        w_cross_key,
-        w_cross_value,
-        w_gate,
-        w_up,
-        w_mod,
-        w_out,
-        w_down,
-    ) = gathered
+    sp_index = lax.axis_index("sp")
+    own_front = jnp.concatenate([w_query, w_key, w_value, w_cross_query], axis=1)
+    own_text = jnp.concatenate([w_cross_key, w_cross_value], axis=1)
+    w_front = jnp.concatenate([own_front, swap_sp(own_front)], axis=0)
+    w_text = jnp.concatenate([own_text, swap_sp(own_text)], axis=0)
+    w_out = lax.all_gather(w_out, "sp", axis=1, tiled=True)
+    w_gate = lax.all_gather(w_gate, "sp", axis=0, tiled=True)
+    w_up = lax.all_gather(w_up, "sp", axis=0, tiled=True)
+    w_down = lax.all_gather(w_down, "sp", axis=1, tiled=True)
     rows_here = tokens.shape[0]
     model_width = tokens.shape[1]
     local_width = w_query.shape[1]
+    text_width = text_states.shape[1]
     heads_here = local_width // HEAD_DIM
     text_rows = text_states.shape[0]
     sequence_len = rows_here * lax.axis_size("sp")
@@ -109,9 +136,20 @@
     group_share = valid_count.astype(jnp.float32) / jnp.sum(counts).astype(jnp.float32)
     row_ids = lax.axis_index("sp") * rows_here + jnp.arange(rows_here)
     valid_rows = (row_ids < valid_count).astype(jnp.float32)[:, None]
-    key_live = (jnp.arange(sequence_len) < valid_count)[None, None, :]
-    part_mod = jnp.dot(condition, w_mod, preferred_element_type=jnp.float32)
-    modulation = lax.all_gather(part_mod, "tp", axis=1, tiled=True)[0]
+    other_ids = (1 - sp_index) * rows_here + jnp.arange(rows_here)
+    key_live = (jnp.concatenate([row_ids, other_ids]) < valid_count)[None, None, :]
+    condition_rows = w_mod.shape[0]
+    own_condition = lax.dynamic_slice_in_dim(
+        condition, sp_index * condition_rows, condition_rows, axis=1
+    )
+    part_mod = jnp.dot(own_condition, w_mod, preferred_element_type=jnp.float32)
+    part_mod = part_mod + swap_sp(part_mod)
+    other_mod = swap_tp(part_mod)
+    tp_first = lax.axis_index("tp") == 0
+    modulation = jnp.concatenate(
+        [jnp.where(tp_first, part_mod, other_mod), jnp.where(tp_first, other_mod, part_mod)],
+        axis=1,
+    )[0]
     scale_attn = modulation[:model_width]
     gate_attn = modulation[model_width : 2 * model_width]
     scale_ffn = modulation[2 * model_width : 3 * model_width]
@@ -120,13 +158,10 @@
     normed_one, factor_one = rms_parts(tokens_wide)
     lift_attn = norm_gains[0] * (1.0 + scale_attn)
     normed_in = (normed_one * lift_attn).astype(jnp.bfloat16)
-    query_pre = jnp.dot(normed_in, w_query, preferred_element_type=jnp.float32).reshape(
-        rows_here, heads_here, HEAD_DIM
-    )
-    key_pre = jnp.dot(normed_in, w_key, preferred_element_type=jnp.float32).reshape(
-        rows_here, heads_here, HEAD_DIM
-    )
-    value_low = jnp.dot(normed_in, w_value, preferred_element_type=jnp.float32).astype(jnp.bfloat16)
+    front = jnp.dot(turn_halves(normed_in), w_front, preferred_element_type=jnp.float32)
+    query_pre = front[:, :local_width].reshape(rows_here, heads_here, HEAD_DIM)
+    key_pre = front[:, local_width : 2 * local_width].reshape(rows_here, heads_here, HEAD_DIM)
+    value_low = front[:, 2 * local_width : 3 * local_width].astype(jnp.bfloat16)
     query_gain = qk_gains[0].reshape(heads_here, HEAD_DIM)
     key_gain = qk_gains[1].reshape(heads_here, HEAD_DIM)
     query_norm, query_factor = rms_parts(query_pre)
@@ -136,10 +171,10 @@
     sine_table = jnp.sin(angles)[:, None, :]
     query_rot = rotate(query_norm * query_gain, cosine_table, sine_table).astype(jnp.bfloat16)
     key_rot = rotate(key_norm * key_gain, cosine_table, sine_table).astype(jnp.bfloat16)
-    key_all, value_all = (
-        lax.all_gather(key_rot.reshape(rows_here, local_width), "sp", axis=0, tiled=True),
-        lax.all_gather(value_low, "sp", axis=0, tiled=True),
-    )
+    own_pair = jnp.concatenate([key_rot.reshape(rows_here, local_width), value_low], axis=1)
+    all_pair = jnp.concatenate([own_pair, swap_sp(own_pair)], axis=0)
+    key_all = all_pair[:, :local_width]
+    value_all = all_pair[:, local_width:]
     key_all = key_all.reshape(sequence_len, heads_here, HEAD_DIM)
     value_all = value_all.reshape(sequence_len, heads_here, HEAD_DIM)
 
@@ -155,20 +190,14 @@
     self_probs = jnp.exp(scores - self_lse).astype(jnp.bfloat16)
     self_mix = jnp.einsum("hqk,khd->qhd", self_probs, value_all, preferred_element_type=jnp.float32)
     cross_query = (
-        jnp.dot(normed_in, w_cross_query, preferred_element_type=jnp.float32)
-        .astype(jnp.bfloat16)
-        .reshape(rows_here, heads_here, HEAD_DIM)
-    )
-    cross_key_low = jnp.dot(text_states, w_cross_key, preferred_element_type=jnp.float32).astype(
-        jnp.bfloat16
-    )
-    cross_value_low = jnp.dot(
-        text_states, w_cross_value, preferred_element_type=jnp.float32
-    ).astype(jnp.bfloat16)
-    cross_keys, cross_values = (
-        lax.all_gather(cross_key_low, "sp", axis=0, tiled=True),
-        lax.all_gather(cross_value_low, "sp", axis=0, tiled=True),
-    )
+        front[:, 3 * local_width :].astype(jnp.bfloat16).reshape(rows_here, heads_here, HEAD_DIM)
+    )
+    own_cross = jnp.dot(
+        turn_halves(text_states), w_text, preferred_element_type=jnp.float32
+    ).astype(jnp.bfloat16)
+    all_cross = jnp.concatenate([own_cross, swap_sp(own_cross)], axis=0)
+    cross_keys = all_cross[:, :local_width]
+    cross_values = all_cross[:, local_width:]
     text_len = cross_keys.shape[0]
     cross_keys = cross_keys.reshape(text_len, heads_here, HEAD_DIM)
     cross_values = cross_values.reshape(text_len, heads_here, HEAD_DIM)
@@ -213,19 +242,22 @@
     grad_reduced = rms_back(grad_out * tanh_ffn * norm_gains[3], down_norm, down_factor).astype(
         jnp.bfloat16
     )
-    grad_w_down = group_share * jnp.einsum(
-        "tf,td->fd", hidden, grad_reduced, preferred_element_type=jnp.float32
-    )
+    grad_w_down = weight_sum(
+        group_share
+        * jnp.einsum("td,tf->df", grad_reduced, hidden, preferred_element_type=jnp.float32)
+    ).T
     grad_hidden = jnp.einsum("td,fd->tf", grad_reduced, w_down, preferred_element_type=jnp.float32)
     grad_up = (grad_hidden * silu_gate).astype(jnp.bfloat16)
     grad_gate_pre = (
         grad_hidden * up_pre * sigmoid_gate * (1.0 + gate_pre * (1.0 - sigmoid_gate))
     ).astype(jnp.bfloat16)
-    grad_w_gate = group_share * jnp.einsum(
-        "tc,tf->cf", normed_mid, grad_gate_pre, preferred_element_type=jnp.float32
-    )
-    grad_w_up = group_share * jnp.einsum(
-        "tc,tf->cf", normed_mid, grad_up, preferred_element_type=jnp.float32
+    grad_w_gate = weight_sum(
+        group_share
+        * jnp.einsum("tc,tf->cf", normed_mid, grad_gate_pre, preferred_element_type=jnp.float32)
+    )
+    grad_w_up = weight_sum(
+        group_share
+        * jnp.einsum("tc,tf->cf", normed_mid, grad_up, preferred_element_type=jnp.float32)
     )
     grad_normed_mid = tp_sum(
         jnp.einsum("tf,cf->tc", grad_gate_pre, w_gate, preferred_element_type=jnp.float32)
@@ -241,9 +273,10 @@
     grad_attended = rms_back(
         grad_middle * tanh_attn * norm_gains[1], attn_norm, attn_factor
     ).astype(jnp.bfloat16)
-    grad_w_out = group_share * jnp.einsum(
-        "th,td->hd", mixed_heads, grad_attended, preferred_element_type=jnp.float32
-    )
+    grad_w_out = weight_sum(
+        group_share
+        * jnp.einsum("td,th->dh", grad_attended, mixed_heads, preferred_element_type=jnp.float32)
+    ).T
     grad_mixed = (
         jnp.einsum("td,hd->th", grad_attended, w_out, preferred_element_type=jnp.float32)
         .astype(jnp.bfloat16)
@@ -277,17 +310,15 @@
     grad_value_rows = jnp.einsum(
         "hqk,qhd->khd", prob_rows, grad_mixed, preferred_element_type=jnp.float32
     )
-    key_grads = lax.psum_scatter(
-        jnp.concatenate(
-            [
-                grad_key_rows.reshape(rows_here * lax.axis_size("sp"), local_width),
-                grad_value_rows.reshape(rows_here * lax.axis_size("sp"), local_width),
-            ],
-            axis=1,
-        ).astype(jnp.bfloat16),
-        "sp",
-        scatter_dimension=0,
-        tiled=True,
+    partial_pair = jnp.concatenate(
+        [
+            grad_key_rows.reshape(2 * rows_here, local_width),
+            grad_value_rows.reshape(2 * rows_here, local_width),
+        ],
+        axis=1,
+    ).astype(jnp.bfloat16)
+    key_grads = partial_pair[:rows_here].astype(jnp.float32) + swap_sp(
+        partial_pair[rows_here:]
     ).astype(jnp.float32)
     grad_key_rot = key_grads[:, :local_width].reshape(rows_here, heads_here, HEAD_DIM)
     grad_value = key_grads[:, local_width:].astype(jnp.bfloat16)
@@ -334,53 +365,34 @@
     grad_value_rows = jnp.einsum(
         "hqk,qhd->khd", prob_rows, grad_cross_mix, preferred_element_type=jnp.float32
     )
-    text_grads_local = lax.psum_scatter(
-        jnp.concatenate(
-            [
-                grad_key_rows.reshape(text_rows * lax.axis_size("sp"), local_width),
-                grad_value_rows.reshape(text_rows * lax.axis_size("sp"), local_width),
-            ],
-            axis=1,
-        ).astype(jnp.bfloat16),
-        "sp",
-        scatter_dimension=0,
-        tiled=True,
+    partial_pair = jnp.concatenate(
+        [
+            grad_key_rows.reshape(2 * text_rows, local_width),
+            grad_value_rows.reshape(2 * text_rows, local_width),
+        ],
+        axis=1,
+    ).astype(jnp.bfloat16)
+    text_grads_local = partial_pair[:text_rows].astype(jnp.float32) + swap_sp(
+        partial_pair[text_rows:]
     ).astype(jnp.float32)
-    grad_cross_key = text_grads_local[:, :local_width].astype(jnp.bfloat16)
-    grad_cross_value = text_grads_local[:, local_width:].astype(jnp.bfloat16)
-    grad_w_cross_key = group_share * jnp.einsum(
-        "tc,tf->cf", text_states, grad_cross_key, preferred_element_type=jnp.float32
-    )
-    grad_w_cross_value = group_share * jnp.einsum(
-        "tc,tf->cf", text_states, grad_cross_value, preferred_element_type=jnp.float32
-    )
-    text_partial = jnp.einsum(
-        "tf,cf->tc", grad_cross_key, w_cross_key, preferred_element_type=jnp.float32
-    ) + jnp.einsum("tf,cf->tc", grad_cross_value, w_cross_value, preferred_element_type=jnp.float32)
-    grad_text = lax.psum_scatter(
-        text_partial.astype(jnp.bfloat16), "tp", scatter_dimension=1, tiled=True
-    ).astype(jnp.float32)
-    grad_w_query = group_share * jnp.einsum(
-        "tc,tf->cf", normed_in, grad_query, preferred_element_type=jnp.float32
-    )
-    grad_w_key = group_share * jnp.einsum(
-        "tc,tf->cf", normed_in, grad_key, preferred_element_type=jnp.float32
-    )
-    grad_w_value = group_share * jnp.einsum(
-        "tc,tf->cf", normed_in, grad_value, preferred_element_type=jnp.float32
-    )
-    grad_w_cross_query = group_share * jnp.einsum(
-        "tc,tf->cf", normed_in, grad_cross_query, preferred_element_type=jnp.float32
-    )
-    input_partial = jnp.einsum("tf,cf->tc", grad_query, w_query, preferred_element_type=jnp.float32)
-    input_partial = input_partial + jnp.einsum(
-        "tf,cf->tc", grad_key, w_key, preferred_element_type=jnp.float32
-    )
-    input_partial = input_partial + jnp.einsum(
-        "tf,cf->tc", grad_value, w_value, preferred_element_type=jnp.float32
-    )
-    input_partial = input_partial + jnp.einsum(
-        "tf,cf->tc", grad_cross_query, w_cross_query, preferred_element_type=jnp.float32
+    text_grads = text_grads_local.astype(jnp.bfloat16)
+    grad_w_text = weight_sum(
+        group_share
+        * jnp.einsum("tc,tf->cf", text_states, text_grads, preferred_element_type=jnp.float32)
+    )
+    text_partial = turn_halves(
+        jnp.einsum("tf,cf->tc", text_grads, w_text, preferred_element_type=jnp.float32)
+    ).astype(jnp.bfloat16)
+    text_half = text_width // 2
+    text_pieces = text_partial.reshape(text_rows, 2, text_half)
+    grad_text = halve(text_pieces, 1, lax.axis_index("tp"), swap_tp)
+    front_grads = jnp.concatenate([grad_query, grad_key, grad_value, grad_cross_query], axis=1)
+    grad_w_front = weight_sum(
+        group_share
+        * jnp.einsum("tc,tf->cf", normed_in, front_grads, preferred_element_type=jnp.float32)
+    )
+    input_partial = turn_halves(
+        jnp.einsum("tf,cf->tc", front_grads, w_front, preferred_element_type=jnp.float32)
     )
     grad_normed_in = tp_sum(input_partial)
     grad_gain_one = jnp.sum(grad_normed_in * normed_one * (1.0 + scale_attn), axis=0)
@@ -393,45 +405,52 @@
     own_modulation = lax.dynamic_slice_in_dim(
         grad_modulation, lax.axis_index("tp") * mod_width, mod_width
     )
-    grad_w_mod = group_share * (
-        condition.astype(jnp.float32).reshape(-1, 1) * own_modulation[None, :]
-    )
-    gain_grads = group_share * jnp.stack(
-        [grad_gain_one, grad_gain_two, grad_gain_three, grad_gain_four]
-    )
-    qk_grads = group_share * jnp.stack([grad_query_gain.reshape(-1), grad_key_gain.reshape(-1)])
-    small_sums = lax.psum((gain_grads, qk_grads, group_share * grad_cross_gate), ("grp", "sp"))
-    reduced_all = (
-        lax.psum_scatter(grad_w_mod, ("grp", "sp"), scatter_dimension=0, tiled=True),
-        lax.psum_scatter(grad_w_query, ("grp", "sp"), scatter_dimension=0, tiled=True),
-        lax.psum_scatter(grad_w_key, ("grp", "sp"), scatter_dimension=0, tiled=True),
-        lax.psum_scatter(grad_w_value, ("grp", "sp"), scatter_dimension=0, tiled=True),
-        lax.psum_scatter(grad_w_out, ("grp", "sp"), scatter_dimension=1, tiled=True),
-        lax.psum_scatter(grad_w_cross_query, ("grp", "sp"), scatter_dimension=0, tiled=True),
-        lax.psum_scatter(grad_w_cross_key, ("grp", "sp"), scatter_dimension=0, tiled=True),
-        lax.psum_scatter(grad_w_cross_value, ("grp", "sp"), scatter_dimension=0, tiled=True),
-        lax.psum_scatter(grad_w_gate, ("grp", "sp"), scatter_dimension=0, tiled=True),
-        lax.psum_scatter(grad_w_up, ("grp", "sp"), scatter_dimension=0, tiled=True),
-        lax.psum_scatter(grad_w_down, ("grp", "sp"), scatter_dimension=1, tiled=True),
+    small = jnp.concatenate(
+        [
+            own_modulation,
+            group_share * jnp.concatenate([grad_gain_one, grad_gain_two]),
+            group_share * jnp.concatenate([grad_gain_three, grad_gain_four]),
+            group_share * jnp.concatenate([grad_query_gain.reshape(-1), grad_key_gain.reshape(-1)]),
+            group_share * grad_cross_gate,
+        ]
+    )
+    small_len = small.shape[0]
+    small = jnp.pad(small, (0, -small_len % 1024)).reshape(-1, 128)
+    small_all = lax.all_gather(small, ("grp", "sp"), axis=0).reshape(
+        2 * counts.shape[0], small.shape[0] * 128
+    )
+    mod_all = jnp.sum(small_all[:, :mod_width].reshape(-1, 2, mod_width), axis=1)
+    gain_sums = jnp.sum(small_all[:, mod_width:small_len], axis=0)
+    gains_end = 4 * model_width
+    qk_end = gains_end + 2 * local_width
+    shares = counts.astype(jnp.float32) / jnp.sum(counts).astype(jnp.float32)
+    block_rows = condition.shape[1] // (2 * counts.shape[0])
+    block_no = 2 * group_no + sp_index
+    condition_all = lax.all_gather(condition, "grp", axis=0, tiled=True)
+    block_condition = lax.dynamic_slice_in_dim(
+        condition_all, block_no * block_rows, block_rows, axis=1
+    ).astype(jnp.float32)
+    grad_w_mod = jnp.einsum(
+        "gc,gf->cf", block_condition, shares[:, None] * mod_all, precision=lax.Precision.HIGHEST
     )
     return (
         output,
         grad_tokens,
         grad_text,
-        reduced_all[0],
-        small_sums[0],
-        small_sums[1],
-        small_sums[2],
-        reduced_all[1],
-        reduced_all[2],
-        reduced_all[3],
-        reduced_all[4],
-        reduced_all[5],
-        reduced_all[6],
-        reduced_all[7],
-        reduced_all[8],
-        reduced_all[9],
-        reduced_all[10],
+        grad_w_mod,
+        gain_sums[:gains_end].reshape(4, model_width),
+        gain_sums[gains_end:qk_end].reshape(2, local_width),
+        gain_sums[qk_end:],
+        grad_w_front[:, :local_width],
+        grad_w_front[:, local_width : 2 * local_width],
+        grad_w_front[:, 2 * local_width : 3 * local_width],
+        grad_w_out,
+        grad_w_front[:, 3 * local_width :],
+        grad_w_text[:, :local_width],
+        grad_w_text[:, local_width:],
+        grad_w_gate,
+        grad_w_up,
+        grad_w_down,
     )
 
 

time: 2080 us -> 1340 us (0.64)
  waiting for transfers between devices: 1440 us -> 383 us
  local copies, waits for them, and re-layouts: 34.6 us -> 260 us
  other arithmetic: 147 us -> 221 us
  matrix products: 359 us -> 309 us
  blocking collectives: 74.6 us -> 110 us
  starting transfers between devices: 3 us -> 32.9 us
    reduce_scatter x13 -> x0, waiting for transfers between devices: 1140 us -> none  [the longest x1 139 us: pair_plan(): lax.psum_scatter(grad_w_mod, ('grp', 'sp'), scatter_dimension=0, tiled=True)]
    ppermute x0 -> x37, waiting for transfers between devices: none -> 381 us  [the longest x18 297 us: weight_sum(): lax.ppermute(sent, 'grp', pairs)]
    psum x4 -> x0, waiting for transfers between devices: 205 us -> none  [tp_sum(): return lax.psum(partial_sum.astype(jnp.bfloat16), 'tp').astype(jnp.float32)]
    all_gather x3 -> x2, blocking collectives: 9.29 us -> 110 us  [the longest x1 79.4 us: pair_plan(): lax.all_gather(small, ('grp', 'sp'), axis=0)]
    dynamic_slice x0 -> x14, local copies, waits for them, and re-layouts: none -> 91.4 us  [the longest x7 51.3 us: halve(): keep_part = lax.dynamic_index_in_dim(values, bit, axis, keepdims=False)]
    all_gather x13 -> x4, waiting for transfers between devices: 89.2 us -> 0.03 us  [the longest x1 0.02 us: pair_plan(): w_gate = lax.all_gather(w_gate, 'sp', axis=0, tiled=True)]
    psum x1 -> x0, blocking collectives: 65.3 us -> none  [pair_plan(): lax.psum((gain_grads, qk_grads, group_share * grad_cross_gate), ('grp', '...]
    convert_element_type x1 -> x22, other arithmetic: 2.18 us -> 49.2 us  [the longest x18 40.6 us: weight_sum(): summed.astype(jnp.bfloat16)]
  transfers between devices with their start and end apart: 31 -> 41, of which waited for: 25 -> 17; matrix products, arithmetic and copies ran while one was open for 16% -> 54% of each run, Pallas kernels for 0% -> 0%
where the time goes in v1:
time: 1340 us; the launch traced here: 1330 us
  waiting for transfers between devices  383 us (29%)
  matrix products  309 us (23%)
  local copies, waits for them, and re-layouts  260 us (19%)
  other arithmetic  221 us (16%)
  blocking collectives  110 us (8%)
  starting transfers between devices  32.9 us (2%)
  between operations  17.2 us (1%)
    ppermute x18, waiting for transfers between devices, weight_sum(): lax.ppermute(sent, 'grp', pairs)  297 us
    ppermute x6, waiting for transfers between devices, swap_tp(): return lax.ppermute(value, 'tp', [(i, i ^ 1) for i in range(size)])  84.2 us
    all_gather x1, blocking collectives, pair_plan(): lax.all_gather(small, ('grp', 'sp'), axis=0)  79.4 us
    unnamed x281, local copies, waits for them, and re-layouts  59 us
    dynamic_slice x7, local copies, waits for them, and re-layouts, halve(): keep_part = lax.dynamic_index_in_dim(values, bit, axis, keepdims=False)  51.3 us
    convert_element_type x1, other arithmetic, pair_plan(): grad_scores = (probs_wide * (grad_probs - jnp.sum(probs_wide * grad_probs...  45.5 us
    convert_element_type x18, other arithmetic, weight_sum(): summed.astype(jnp.bfloat16)  40.6 us
    dynamic_slice x6, local copies, waits for them, and re-layouts, halve(): sent_part = lax.dynamic_index_in_dim(values, 1 - bit, axis, keepdims=False)  39.4 us
  transfers between devices with their start and end apart: 41, of which 17 were waited for; matrix products, arithmetic and copies ran while one was open for 54% of the time, Pallas kernels for 0%

profile of v1, /device:TPU:0, one launch (start us, length us, event | category | flops | bytes accessed | tf_op | source)
XLA Modules:
  0.0 1333.2 jit_solution(5612158735252354299)
XLA Ops:
  32.3 14.2 %fusion.116 = (bf16[768,3072]{1,0:T(8,128)(2,1)}, f32[768,3072]{1,0:T(8,128)}) fusion(bf16[768,3072]{1,0:T(8,128)(2,1)} %collective-permute-done.2, bf16[768,3072]{1,0:T(8,128)(2,1)} %constant_dynamic-update-slice_fusion, bf16[768,1536]{1,0:T(8,128)(2,1)S(1)} %fusion.19, bf16[768,768]{1,0:T(8,128)(2,1)S(1)} %get-tuple-element.94, ...), kind=kOutput, calls=%fused_computation.346 | convolution fusion | flops 7274889216 | bytes 28311552 | tf_op jit(solution)/shard_map/dot_general | solution.py:161
  99.3 10.0 pad_maximum_fusion.6
  116.1 22.7 %fusion = (f32[12,768]{1,0:T(8,128)S(1)}, f32[12,768,1536]{2,1,0:T(8,128)}) fusion(pred[1536]{0:T(1024)(128)(4,1)S(1)} %add_compare_fusion, bf16[1536,12,64]{0,2,1:T(8,128)(2,1)} %bitcast.267, bf16[768,12,32]{0,2,1:T(8,128)(2,1)} %get-tuple-element.82, bf16[768,12,32]{0,2,1:T(8,128)(2,1)S(1)} %get-tuple-element.81), kind=kOutput, calls=%fused_computation.5 | convolution fusion | flops 1856756736 | bytes 60200448 | tf_op jit(solution)/shard_map/qhd,khd->hqk/dot_general | solution.py:183
  138.9 18.4 %exponential_reduce_fusion = f32[12,768]{1,0:T(8,128)S(1)} fusion(f32[12,768,1536]{2,1,0:T(8,128)} %get-tuple-element.123, f32[12,768]{1,0:T(8,128)S(1)} %get-tuple-element.122, pred[1536]{0:T(1024)(128)(4,1)S(1)} %add_compare_fusion), kind=kLoop, calls=%fused_computation.3 | loop fusion | flops 56613888 | bytes 56698368 | tf_op jit(solution)/shard_map/reduce_sum | solution.py:45
  161.6 22.7 %fusion.47 = bf16[768,12,64]{0,2,1:T(8,128)(2,1)} fusion(f32[12,64,768]{2,1,0:T(8,128)} %fusion.63, bf16[1536,12,64]{0,2,1:T(8,128)(2,1)} %bitcast.289, f32[12]{0:T(128)S(1)} %tanh.15, f32[12,768,1536]{2,1,0:T(8,128)} %get-tuple-element.123, f32[12,768]{1,0:T(8,128)S(1)} %log_add_fusion.1, pred[1536]{0:T(1024)(128)(4,1)S(1)} %add_compare_fusion), kind=kOutput, calls=%fused_computation.138 | convolution fusion | flops 1870331904 | bytes 62559792 | tf_op jit(solution)/shard_map/hqk,khd->qhd/dot_general | solution.py:191
  191.9 52.1 %collective-permute-done.6 = bf16[768,1536]{1,0:T(8,128)(2,1)} collective-permute-done((bf16[768,1536]{1,0:T(8,128)(2,1)}, bf16[768,1536]{1,0:T(8,128)(2,1)}, u32[]{:S(2)}, u32[]{:S(2)}) %collective-permute-start.6) | collective-permute-done | bytes 2359328 | tf_op jit(solution)/shard_map/ppermute | solution.py:55
  254.0 10.5 fusion.117
  264.5 11.6 multiply_convert_fusion.9
  276.2 9.1 convolution_convert_fusion.1
  288.3 30.9 %all-gather = bf16[8,1,1024]{2,1,0:T(2,128)(2,1)S(1)} all-gather(bf16[1,1,1024]{2,1,0:T(2,128)(2,1)S(1)} %bitcast.312), channel_id=1, replica_groups=mesh['grp'=8,'tp'=2,'sp'=2] {'grp'}, dimensions={0}, use_global_device_ids=true | all-gather | bytes 18432 | tf_op jit(solution)/shard_map/all_gather | solution.py:429
  325.5 13.1 collective-permute-done.7
  347.0 6.2 multiply_convert_fusion.13
  353.1 12.9 multiply_convert_fusion.7
  366.1 7.1 fusion.118
  373.3 9.0 add_convert_fusion
  416.6 17.9 %collective-permute-done.8 = bf16[768,1536]{1,0:T(8,128)(2,1)S(1)} collective-permute-done((bf16[768,1536]{1,0:T(8,128)(2,1)S(1)}, bf16[768,1536]{1,0:T(8,128)(2,1)S(1)}, u32[]{:S(2)}, u32[]{:S(2)}) %collective-permute-start.8) | collective-permute-done | bytes 2359328 | tf_op jit(solution)/shard_map/ppermute | solution.py:55
  437.6 6.7 multiply_reduce_fusion.5
  458.6 23.4 %convolution_convert_fusion = bf16[12,64,1536]{2,1,0:T(8,128)(2,1)} fusion(bf16[768,12,64]{0,2,1:T(8,128)(2,1)S(1)} %bitcast.275, f32[12,768,1536]{2,1,0:T(8,128)} %get-tuple-element.123, f32[12,768]{1,0:T(8,128)S(1)} %copy-done.55, pred[1536]{0:T(1024)(128)(4,1)S(1)} %copy-done.75), kind=kOutput, calls=%fused_computation.100 | convolution fusion | flops 1869742080 | bytes 60200448 | tf_op jit(solution)/shard_map/hqk,qhd->khd/dot_general | solution.py:310
  481.9 7.2 multiply_reduce_fusion.1
  489.1 10.8 multiply_convert_fusion.6
  506.6 38.3 %multiply_reduce_fusion = (f32[12,768]{1,0:T(8,128)S(1)}, f32[12,768,1536]{2,1,0:T(8,128)}) fusion(f32[12,768,1536]{2,1,0:T(8,128)} %get-tuple-element.123, f32[12,768]{1,0:T(8,128)S(1)} %copy-done.55, pred[1536]{0:T(1024)(128)(4,1)S(1)} %copy-done.75, bf16[768,12,64]{0,2,1:T(8,128)(2,1)S(1)} %bitcast.277, bf16[1536,12,64]{0,2,1:T(8,128)(2,1)S(1)} %bitcast.290), kind=kOutput, calls=%fused_computation.1 | convolution fusion | flops 1882708992 | bytes 116860416 | tf_op jit(solution)/shard_map/qhd,khd->hqk/dot_general | solution.py:294
  544.9 45.5 %multiply_convert_fusion = bf16[12,768,1536]{2,1,0:T(8,128)(2,1)} fusion(f32[12,768,1536]{2,1,0:T(8,128)} %get-tuple-element.129, f32[12,768,1536]{2,1,0:T(8,128)} %get-tuple-element.123, f32[12,768]{1,0:T(8,128)S(1)} %get-tuple-element.128, f32[12,768]{1,0:T(8,128)S(1)} %copy-done.55, pred[1536]{0:T(1024)(128)(4,1)S(1)} %copy-done.75), kind=kLoop, calls=%fused_computation | loop fusion | flops 84934656 | bytes 141633024 | tf_op jit(solution)/shard_map/convert_element_type | solution.py:299
  590.4 15.4 %multiply_bitcast_fusion = f32[768,12,64]{0,2,1:T(8,128)} fusion(bf16[1536,12,64]{0,2,1:T(8,128)(2,1)S(1)} %bitcast.268, bf16[12,768,1536]{2,1,0:T(8,128)(2,1)} %multiply_convert_fusion), kind=kOutput, calls=%fused_computation.147 | convolution fusion | flops 1812529152 | bytes 33030144 | tf_op jit(solution)/shard_map/hqk,khd->qhd/dot_general | solution.py:301
  605.9 15.8 %multiply_convert_fusion.11 = bf16[12,64,1536]{2,1,0:T(8,128)(2,1)} fusion(bf16[12,768,1536]{2,1,0:T(8,128)(2,1)} %multiply_convert_fusion, bf16[768,12,32]{0,2,1:T(8,128)(2,1)} %get-tuple-element.82, bf16[768,12,32]{0,2,1:T(8,128)(2,1)S(1)} %copy-done.37), kind=kOutput, calls=%fused_computation.76 | convolution fusion | flops 1816657920 | bytes 31850496 | tf_op jit(solution)/shard_map/hqk,qhd->khd/dot_general | solution.py:307
  637.8 8.4 fusion.5
  646.3 7.5 fusion.2
  663.5 21.0 %reshape.465 = bf16[2,2,2,2,256,1536]{4,3,2,1,0,5:T(2,128)(2,1)} reshape(bf16[4096,1536]{0,1:T(8,128)(2,1)} %fusion.2) | data formatting | bytes 25165824 | tf_op jit(solution)/shard_map/reshape | solution.py:80
  684.5 29.2 %constant_dynamic-slice_fusion.7 = (bf16[2,2,2,1,256,1536]{4,3,2,1,0,5:T(2,128)(2,1)}, bf16[2,2,2,1,256,1536]{4,3,2,1,0,5:T(2,128)(2,1)}) fusion(bf16[2,2,2,2,256,1536]{4,3,2,1,0,5:T(2,128)(2,1)} %reshape.465, s32[]{:T(128)S(6)} %select_n.161, s32[]{:T(128)S(6)} %select_n.162), kind=kLoop, calls=%fused_computation.261 | loop fusion | bytes 25165832 | tf_op jit(solution)/shard_map/jit(dynamic_index_in_dim)/dynamic_slice | solution.py:70
  713.7 29.5 %copy.168 = bf16[2,2,2,1,256,1536]{5,4,1,0,2,3:T(8,128)(2,1)} copy(bf16[2,2,2,1,256,1536]{4,3,2,1,0,5:T(2,128)(2,1)} %get-tuple-element.57) | data formatting | bytes 12582912
  743.2 29.7 %copy.152 = bf16[2,2,2,1,256,1536]{5,4,1,0,2,3:T(8,128)(2,1)} copy(bf16[2,2,2,1,256,1536]{4,3,2,1,0,5:T(2,128)(2,1)} %get-tuple-element.58) | data formatting | bytes 12582912 | tf_op jit(solution)/shard_map/jit(dynamic_index_in_dim)/dynamic_slice | solution.py:71
  793.8 40.9 %collective-permute-done.18 = bf16[2,2,96,768]{3,2,1,0:T(8,128)(2,1)S(1)} collective-permute-done((bf16[2,2,96,768]{3,2,1,0:T(8,128)(2,1)S(1)}, bf16[2,2,96,768]{3,2,1,0:T(8,128)(2,1)S(1)}, u32[]{:S(2)}, u32[]{:S(2)}) %collective-permute-start.18) | collective-permute-done | bytes 589856 | tf_op jit(solution)/shard_map/ppermute | solution.py:90
  840.2 10.3 collective-permute-done.19
  887.9 6.6 multiply_reduce_fusion.18
  896.0 11.0 multiply_convert_fusion.2
  907.0 12.6 fusion.17
  921.2 8.7 constant_dynamic-slice_fusion.11
  943.1 47.6 %collective-permute-done.31 = bf16[2,96,2048]{2,1,0:T(8,128)(2,1)S(1)} collective-permute-done((bf16[2,96,2048]{2,1,0:T(8,128)(2,1)S(1)}, bf16[2,96,2048]{2,1,0:T(8,128)(2,1)S(1)}, u32[]{:S(2)}, u32[]{:S(2)}) %collective-permute-start.31) | collective-permute-done | bytes 786464 | tf_op jit(solution)/shard_map/ppermute | solution.py:90
  990.9 33.4 %collective-permute-done.35 = bf16[2,96,2048]{2,1,0:T(8,128)(2,1)S(1)} collective-permute-done((bf16[2,96,2048]{2,1,0:T(8,128)(2,1)S(1)}, bf16[2,96,2048]{2,1,0:T(8,128)(2,1)S(1)}, u32[]{:S(2)}, u32[]{:S(2)}) %collective-permute-start.35) | collective-permute-done | bytes 786464 | tf_op jit(solution)/shard_map/ppermute | solution.py:90
  1024.6 15.8 %collective-permute-done.27 = bf16[2,96,2048]{2,1,0:T(8,128)(2,1)S(1)} collective-permute-done((bf16[2,96,2048]{2,1,0:T(8,128)(2,1)S(1)}, bf16[2,96,2048]{2,1,0:T(8,128)(2,1)S(1)}, u32[]{:S(2)}, u32[]{:S(2)}) %collective-permute-start.27) | collective-permute-done | bytes 786464 | tf_op jit(solution)/shard_map/ppermute | solution.py:90
  1041.3 7.6 collective-permute-done.32
  1049.8 7.4 collective-permute-done.36
  1058.3 7.4 collective-permute-done.28
  1081.2 9.1 fusion.3
  1099.1 35.2 %collective-permute-done.14 = bf16[2,2,96,3072]{3,2,1,0:T(8,128)(2,1)} collective-permute-done((bf16[2,2,96,3072]{3,2,1,0:T(8,128)(2,1)}, bf16[2,2,96,3072]{3,2,1,0:T(8,128)(2,1)}, u32[]{:S(2)}, u32[]{:S(2)}) %collective-permute-start.14) | collective-permute-done | bytes 2359328 | tf_op jit(solution)/shard_map/ppermute | solution.py:90
  1139.6 61.1 %collective-permute-done.22 = bf16[2,2,256,1536]{3,2,1,0:T(8,128)(2,1)S(1)} collective-permute-done((bf16[2,2,256,1536]{3,2,1,0:T(8,128)(2,1)S(1)}, bf16[2,2,256,1536]{3,2,1,0:T(8,128)(2,1)S(1)}, u32[]{:S(2)}, u32[]{:S(2)}) %collective-permute-start.22) | collective-permute-done | bytes 3145760 | tf_op jit(solution)/shard_map/ppermute | solution.py:90
  1204.3 79.4 %all_gather.23 = f32[16,88,128]{2,1,0:T(8,128)S(1)} all-gather(f32[1,88,128]{2,1,0:T(8,128)S(1)} %pad_bitcast_fusion), channel_id=1, replica_groups=mesh['grp'=8,'tp'=2,'sp'=2] {'grp','sp'}, dimensions={0}, use_global_device_ids=true | all-gather | bytes 765952 | tf_op jit(solution)/shard_map/all_gather | solution.py:419
  1296.2 12.2 collective-permute-done.16
  1309.6 15.3 %collective-permute-done.24 = bf16[256,1536]{1,0:T(8,128)(2,1)S(1)} collective-permute-done((bf16[256,1536]{1,0:T(8,128)(2,1)S(1)}, bf16[256,1536]{1,0:T(8,128)(2,1)S(1)}, u32[]{:S(2)}, u32[]{:S(2)}) %collective-permute-start.24) | collective-permute-done | bytes 786464 | tf_op jit(solution)/shard_map/ppermute | solution.py:90
  (538 shorter events, 337.5 us)
Async XLA Ops:
  7.2 177.1 %all-gather.6.cloned.1.call-start = ((), (), s32[]{:S(2)}) async-start(), calls=%async_computation | async-start | bytes 3538944 | tf_op jit(solution)/shard_map/all_gather | solution.py:122
  7.9 246.1 %all-gather.8.cloned.1.call-start = ((), (), s32[]{:S(2)}) async-start(), calls=%async_computation.1 | async-start | bytes 9437184 | tf_op jit(solution)/shard_map/all_gather | solution.py:123
  8.7 255.8 %all-gather.10.cloned.1.call-start = ((), (), s32[]{:S(2)}) async-start(), calls=%async_computation.2 | async-start | bytes 9437184 | tf_op jit(solution)/shard_map/all_gather | solution.py:124
  14.6 17.8 %collective-permute-start.2 = (bf16[768,3072]{1,0:T(8,128)(2,1)}, bf16[768,3072]{1,0:T(8,128)(2,1)}, u32[]{:S(2)}, u32[]{:S(2)}) collective-permute-start(bf16[768,3072]{1,0:T(8,128)(2,1)} %constant_dynamic-update-slice_fusion), channel_id=1, source_target_pairs={{0,1},{1,0},{2,3},{3,2},{4,5},{5,4},{6,7},{7,6},{8,9},{9,8},{10,11... | collective-permute-start | bytes 14155784 | tf_op jit(solution)/shard_map/ppermute | solution.py:50
  15.6 11.0 collective-permute-start
  20.9 53.0 %collective-permute-start.4 = (bf16[2048,1536]{1,0:T(8,128)(2,1)}, bf16[2048,1536]{1,0:T(8,128)(2,1)}, u32[]{:S(2)}, u32[]{:S(2)}) collective-permute-start(bf16[2048,1536]{1,0:T(8,128)(2,1)} %constant_dynamic-update-slice_fusion.4), channel_id=1, source_target_pairs={{0,1},{1,0},{2,3},{3,2},{4,5},{5,4},{6,7},{7,6},{8,9},{9,8},{10,11... | collective-permute-start | bytes 18874376 | tf_op jit(solution)/shard_map/ppermute | solution.py:50
  21.0 255.2 %all-gather.12.cloned.1.call-start = ((), (), s32[]{:S(2)}) async-start(), calls=%async_computation.3 | async-start | bytes 9437184 | tf_op jit(solution)/shard_map/all_gather | solution.py:125
  26.6 4.1 collective-permute-start.1
  63.2 257.9 %copy-start.67 = (f32[768,12]{0,1:T(8,128)}, f32[768,12]{0,1:T(8,128)S(1)}, u32[]{:S(2)}) copy-start(f32[768,12]{0,1:T(8,128)S(1)} %add_rsqrt_fusion) | copy-start | bytes 110596
  63.2 260.1 %copy-start.69 = (f32[768,12]{0,1:T(8,128)}, f32[768,12]{0,1:T(8,128)S(1)}, u32[]{:S(2)}) copy-start(f32[768,12]{0,1:T(8,128)S(1)} %add_rsqrt_fusion.1) | copy-start | bytes 110596
  73.9 25.4 %collective-permute-start.3 = (bf16[768,1536]{1,0:T(8,128)(2,1)}, bf16[768,1536]{1,0:T(8,128)(2,1)}, u32[]{:S(2)}, u32[]{:S(2)}) collective-permute-start(bf16[768,1536]{1,0:T(8,128)(2,1)} %pad_maximum_fusion.11), channel_id=1, source_target_pairs={{0,1},{1,0},{2,3},{3,2},{4,5},{5,4},{6,7},{7,6},{8,9},{9,8},{10,11... | collective-permute-start | bytes 7077896 | tf_op jit(solution)/shard_map/ppermute | solution.py:50
  80.7 4.0 collective-permute-start.5
  80.8 80.8 %copy-start.110 = (f32[12]{0:T(128)}, f32[12]{0:T(128)S(1)}, u32[]{:S(2)}) copy-start(f32[12]{0:T(128)S(1)} %tanh.15) | copy-start | bytes 148
  189.8 54.3 %collective-permute-start.6 = (bf16[768,1536]{1,0:T(8,128)(2,1)}, bf16[768,1536]{1,0:T(8,128)(2,1)}, u32[]{:S(2)}, u32[]{:S(2)}) collective-permute-start(bf16[768,1536]{1,0:T(8,128)(2,1)} %convolution_convert_fusion.2), channel_id=1, source_target_pairs={{0,2},{2,0},{1,3},{3,1},{4,6},{6,4},{5,7},{7,5},{8,10},{10,8},{9,1... | collective-permute-start | bytes 7077896 | tf_op jit(solution)/shard_map/ppermute | solution.py:55
  285.3 53.4 %collective-permute-start.7 = (bf16[768,1536]{1,0:T(8,128)(2,1)}, bf16[768,1536]{1,0:T(8,128)(2,1)}, u32[]{:S(2)}, u32[]{:S(2)}) collective-permute-start(bf16[768,1536]{1,0:T(8,128)(2,1)} %convolution_convert_fusion.1), channel_id=1, source_target_pairs={{0,2},{2,0},{1,3},{3,1},{4,6},{6,4},{5,7},{7,5},{8,10},{10,8},{9,1... | collective-permute-start | bytes 7077896 | tf_op jit(solution)/shard_map/ppermute | solution.py:55
  382.2 52.3 %collective-permute-start.8 = (bf16[768,1536]{1,0:T(8,128)(2,1)S(1)}, bf16[768,1536]{1,0:T(8,128)(2,1)S(1)}, u32[]{:S(2)}, u32[]{:S(2)}) collective-permute-start(bf16[768,1536]{1,0:T(8,128)(2,1)S(1)} %add_convert_fusion), channel_id=1, source_target_pairs={{0,2},{2,0},{1,3},{3,1},{4,6},{6,4},{5,7},{7,5},{8,10},{10,8},{9,1... | collective-permute-start | bytes 7077896 | tf_op jit(solution)/shard_map/ppermute | solution.py:55
  415.5 357.4 %collective-permute-start.29 = (bf16[2,2,2,96,2048]{4,3,1,0,2:T(8,128)(2,1)}, bf16[2,2,2,96,2048]{4,3,1,0,2:T(8,128)(2,1)}, u32[]{:S(2)}, u32[]{:S(2)}) collective-permute-start(bf16[2,2,2,96,2048]{4,3,1,0,2:T(8,128)(2,1)} %bitcast.250), channel_id=1, source_target_pairs={{0,1},{1,0},{2,3},{3,2},{4,5},{5,4},{6,7},{7,6},{8,9},{9,8},{10,11... | collective-permute-start | bytes 9437192 | tf_op jit(solution)/shard_map/ppermute | solution.py:50
  415.5 364.2 %collective-permute-start.33 = (bf16[2,2,2,96,2048]{4,3,1,0,2:T(8,128)(2,1)}, bf16[2,2,2,96,2048]{4,3,1,0,2:T(8,128)(2,1)}, u32[]{:S(2)}, u32[]{:S(2)}) collective-permute-start(bf16[2,2,2,96,2048]{4,3,1,0,2:T(8,128)(2,1)} %bitcast.249), channel_id=1, source_target_pairs={{0,1},{1,0},{2,3},{3,2},{4,5},{5,4},{6,7},{7,6},{8,9},{9,8},{10,11... | collective-permute-start | bytes 9437192 | tf_op jit(solution)/shard_map/ppermute | solution.py:50
  416.0 373.0 %collective-permute-start.25 = (bf16[2,2,2,96,2048]{4,3,1,0,2:T(8,128)(2,1)}, bf16[2,2,2,96,2048]{4,3,1,0,2:T(8,128)(2,1)}, u32[]{:S(2)}, u32[]{:S(2)}) collective-permute-start(bf16[2,2,2,96,2048]{4,3,1,0,2:T(8,128)(2,1)} %bitcast.251), channel_id=1, source_target_pairs={{0,1},{1,0},{2,3},{3,2},{4,5},{5,4},{6,7},{7,6},{8,9},{9,8},{10,11... | collective-permute-start | bytes 9437192 | tf_op jit(solution)/shard_map/ppermute | solution.py:50
  622.5 15.3 %collective-permute-start.11 = (bf16[128,1536]{0,1:T(8,128)(2,1)}, bf16[128,1536]{0,1:T(8,128)(2,1)S(1)}, u32[]{:S(2)}, u32[]{:S(2)}) collective-permute-start(bf16[128,1536]{0,1:T(8,128)(2,1)} %pad_maximum_fusion.20), channel_id=1, source_target_pairs={{0,1},{1,0},{2,3},{3,2},{4,5},{5,4},{6,7},{7,6},{8,9},{9,8},{10,11... | collective-permute-start | bytes 1179656 | tf_op jit(solution)/shard_map/ppermute | solution.py:50
  624.8 160.5 %collective-permute-start.17 = (bf16[2,2,2,96,768]{4,3,1,0,2:T(8,128)(2,1)}, bf16[2,2,2,96,768]{4,3,1,0,2:T(8,128)(2,1)}, u32[]{:S(2)}, u32[]{:S(2)}) collective-permute-start(bf16[2,2,2,96,768]{4,3,1,0,2:T(8,128)(2,1)} %bitcast.252), channel_id=1, source_target_pairs={{0,1},{1,0},{2,3},{3,2},{4,5},{5,4},{6,7},{7,6},{8,9},{9,8},{10,11... | collective-permute-start | bytes 3538952 | tf_op jit(solution)/shard_map/ppermute | solution.py:50
  637.8 220.7 %collective-permute-start.9 = (bf16[768,1536]{1,0:T(8,128)(2,1)}, bf16[768,1536]{1,0:T(8,128)(2,1)}, u32[]{:S(2)}, u32[]{:S(2)}) collective-permute-start(bf16[768,1536]{1,0:T(8,128)(2,1)} %pad_maximum_fusion.10), channel_id=1, source_target_pairs={{0,1},{1,0},{2,3},{3,2},{4,5},{5,4},{6,7},{7,6},{8,9},{9,8},{10,11... | collective-permute-start | bytes 7077896 | tf_op jit(solution)/shard_map/ppermute | solution.py:50
  772.9 79.1 %collective-permute-start.12 = (bf16[128,2048]{1,0:T(8,128)(2,1)}, bf16[128,2048]{1,0:T(8,128)(2,1)S(1)}, u32[]{:S(2)}, u32[]{:S(2)}) collective-permute-start(bf16[128,2048]{1,0:T(8,128)(2,1)} %bitcast.254), channel_id=1, source_target_pairs={{0,2},{2,0},{1,3},{3,1},{4,6},{6,4},{5,7},{7,5},{8,10},{10,8},{9,1... | collective-permute-start | bytes 1572872 | tf_op jit(solution)/shard_map/ppermute | solution.py:55
  779.6 301.6 %collective-permute-start.21 = (bf16[2,2,2,256,1536]{4,3,1,0,2:T(8,128)(2,1)}, bf16[2,2,2,256,1536]{4,3,1,0,2:T(8,128)(2,1)}, u32[]{:S(2)}, u32[]{:S(2)}) collective-permute-start(bf16[2,2,2,256,1536]{4,3,1,0,2:T(8,128)(2,1)} %bitcast.57), channel_id=1, source_target_pairs={{0,1},{1,0},{2,3},{3,2},{4,5},{5,4},{6,7},{7,6},{8,9},{9,8},{10,11... | collective-permute-start | bytes 18874376 | tf_op jit(solution)/shard_map/ppermute | solution.py:50
  785.3 147.6 %collective-permute-start.30 = (bf16[2,2,96,2048]{3,2,1,0:T(8,128)(2,1)}, bf16[2,2,96,2048]{3,2,1,0:T(8,128)(2,1)}, u32[]{:S(2)}, u32[]{:S(2)}) collective-permute-start(bf16[2,2,96,2048]{3,2,1,0:T(8,128)(2,1)} %dynamic-slice_bitcast_fusion.3), channel_id=1, source_target_pairs={{0,4},{4,0},{8,12},{12,8},{16,20},{20,16},{24,28},{28,24},{1,5},{5... | collective-permute-start | bytes 4718600 | tf_op jit(solution)/shard_map/ppermute | solution.py:90
  789.0 45.6 %collective-permute-start.18 = (bf16[2,2,96,768]{3,2,1,0:T(8,128)(2,1)S(1)}, bf16[2,2,96,768]{3,2,1,0:T(8,128)(2,1)S(1)}, u32[]{:S(2)}, u32[]{:S(2)}) collective-permute-start(bf16[2,2,96,768]{3,2,1,0:T(8,128)(2,1)S(1)} %dynamic-slice_bitcast_fusion.11), channel_id=1, source_target_pairs={{0,4},{4,0},{8,12},{12,8},{16,20},{20,16},{24,28},{28,24},{1,5},{5... | collective-permute-start | bytes 1769480 | tf_op jit(solution)/shard_map/ppermute | solution.py:90
  834.9 15.6 %collective-permute-start.19 = (bf16[2,96,768]{2,1,0:T(8,128)(2,1)S(1)}, bf16[2,96,768]{2,1,0:T(8,128)(2,1)S(1)}, u32[]{:S(2)}, u32[]{:S(2)}) collective-permute-start(bf16[2,96,768]{2,1,0:T(8,128)(2,1)S(1)} %dynamic-slice_bitcast_fusion.16), channel_id=1, source_target_pairs={{0,16},{4,20},{8,24},{12,28},{16,0},{20,4},{24,8},{28,12},{1,17},{... | collective-permute-start | bytes 884744 | tf_op jit(solution)/shard_map/ppermute | solution.py:90
  850.4 85.1 %collective-permute-start.34 = (bf16[2,2,96,2048]{3,2,1,0:T(8,128)(2,1)}, bf16[2,2,96,2048]{3,2,1,0:T(8,128)(2,1)}, u32[]{:S(2)}, u32[]{:S(2)}) collective-permute-start(bf16[2,2,96,2048]{3,2,1,0:T(8,128)(2,1)} %dynamic-slice_bitcast_fusion.2), channel_id=1, source_target_pairs={{0,4},{4,0},{8,12},{12,8},{16,20},{20,16},{24,28},{28,24},{1,5},{5... | collective-permute-start | bytes 4718600 | tf_op jit(solution)/shard_map/ppermute | solution.py:90
  852.1 5.2 collective-permute-start.20
  857.3 82.9 %collective-permute-start.26 = (bf16[2,2,96,2048]{3,2,1,0:T(8,128)(2,1)}, bf16[2,2,96,2048]{3,2,1,0:T(8,128)(2,1)}, u32[]{:S(2)}, u32[]{:S(2)}) collective-permute-start(bf16[2,2,96,2048]{3,2,1,0:T(8,128)(2,1)} %dynamic-slice_bitcast_fusion.4), channel_id=1, source_target_pairs={{0,4},{4,0},{8,12},{12,8},{16,20},{20,16},{24,28},{28,24},{1,5},{5... | collective-permute-start | bytes 4718600 | tf_op jit(solution)/shard_map/ppermute | solution.py:90
  920.4 146.2 %collective-permute-start.10 = (bf16[768,1536]{1,0:T(8,128)(2,1)S(1)}, bf16[768,1536]{1,0:T(8,128)(2,1)S(1)}, u32[]{:S(2)}, u32[]{:S(2)}) collective-permute-start(bf16[768,1536]{1,0:T(8,128)(2,1)S(1)} %fusion.25), channel_id=1, source_target_pairs={{0,2},{2,0},{1,3},{3,1},{4,6},{6,4},{5,7},{7,5},{8,10},{10,8},{9,1... | collective-permute-start | bytes 7077896 | tf_op jit(solution)/shard_map/ppermute | solution.py:55
  933.0 136.6 %collective-permute-start.13 = (bf16[2,2,2,96,3072]{4,3,1,0,2:T(8,128)(2,1)S(1)}, bf16[2,2,2,96,3072]{4,3,1,0,2:T(8,128)(2,1)S(1)}, u32[]{:S(2)}, u32[]{:S(2)}) collective-permute-start(bf16[2,2,2,96,3072]{4,3,1,0,2:T(8,128)(2,1)S(1)} %bitcast.294), channel_id=1, source_target_pairs={{0,1},{1,0},{2,3},{3,2},{4,5},{5,4},{6,7},{7,6},{8,9},{9,8},{10,11... | collective-permute-start | bytes 14155784 | tf_op jit(solution)/shard_map/ppermute | solution.py:50
  935.5 55.1 %collective-permute-start.31 = (bf16[2,96,2048]{2,1,0:T(8,128)(2,1)S(1)}, bf16[2,96,2048]{2,1,0:T(8,128)(2,1)S(1)}, u32[]{:S(2)}, u32[]{:S(2)}) collective-permute-start(bf16[2,96,2048]{2,1,0:T(8,128)(2,1)S(1)} %dynamic-slice_bitcast_fusion.8), channel_id=1, source_target_pairs={{0,16},{4,20},{8,24},{12,28},{16,0},{20,4},{24,8},{28,12},{1,17},{... | collective-permute-start | bytes 2359304 | tf_op jit(solution)/shard_map/ppermute | solution.py:90
  940.2 84.2 %collective-permute-start.35 = (bf16[2,96,2048]{2,1,0:T(8,128)(2,1)S(1)}, bf16[2,96,2048]{2,1,0:T(8,128)(2,1)S(1)}, u32[]{:S(2)}, u32[]{:S(2)}) collective-permute-start(bf16[2,96,2048]{2,1,0:T(8,128)(2,1)S(1)} %dynamic-slice_bitcast_fusion.7), channel_id=1, source_target_pairs={{0,16},{4,20},{8,24},{12,28},{16,0},{20,4},{24,8},{28,12},{1,17},{... | collective-permute-start | bytes 2359304 | tf_op jit(solution)/shard_map/ppermute | solution.py:90
  990.6 49.8 %collective-permute-start.27 = (bf16[2,96,2048]{2,1,0:T(8,128)(2,1)S(1)}, bf16[2,96,2048]{2,1,0:T(8,128)(2,1)S(1)}, u32[]{:S(2)}, u32[]{:S(2)}) collective-permute-start(bf16[2,96,2048]{2,1,0:T(8,128)(2,1)S(1)} %dynamic-slice_bitcast_fusion.9), channel_id=1, source_target_pairs={{0,16},{4,20},{8,24},{12,28},{16,0},{20,4},{24,8},{28,12},{1,17},{... | collective-permute-start | bytes 2359304 | tf_op jit(solution)/shard_map/ppermute | solution.py:90
  1024.3 24.5 %collective-permute-start.32 = (bf16[96,2048]{1,0:T(8,128)(2,1)S(1)}, bf16[96,2048]{1,0:T(8,128)(2,1)S(1)}, u32[]{:S(2)}, u32[]{:S(2)}) collective-permute-start(bf16[96,2048]{1,0:T(8,128)(2,1)S(1)} %dynamic-slice_bitcast_fusion.14), channel_id=1, source_target_pairs={{0,8},{4,12},{8,0},{12,4},{16,24},{20,28},{24,16},{28,20},{1,9},{5... | collective-permute-start | bytes 1179656 | tf_op jit(solution)/shard_map/ppermute | solution.py:90
  1040.4 16.8 %collective-permute-start.36 = (bf16[96,2048]{1,0:T(8,128)(2,1)S(1)}, bf16[96,2048]{1,0:T(8,128)(2,1)S(1)}, u32[]{:S(2)}, u32[]{:S(2)}) collective-permute-start(bf16[96,2048]{1,0:T(8,128)(2,1)S(1)} %dynamic-slice_bitcast_fusion.13), channel_id=1, source_target_pairs={{0,8},{4,12},{8,0},{12,4},{16,24},{20,28},{24,16},{28,20},{1,9},{5... | collective-permute-start | bytes 1179656 | tf_op jit(solution)/shard_map/ppermute | solution.py:90
  1048.9 16.8 %collective-permute-start.28 = (bf16[96,2048]{1,0:T(8,128)(2,1)S(1)}, bf16[96,2048]{1,0:T(8,128)(2,1)S(1)}, u32[]{:S(2)}, u32[]{:S(2)}) collective-permute-start(bf16[96,2048]{1,0:T(8,128)(2,1)S(1)} %dynamic-slice_bitcast_fusion.15), channel_id=1, source_target_pairs={{0,8},{4,12},{8,0},{12,4},{16,24},{20,28},{24,16},{28,20},{1,9},{5... | collective-permute-start | bytes 1179656 | tf_op jit(solution)/shard_map/ppermute | solution.py:90
  1079.9 54.4 %collective-permute-start.14 = (bf16[2,2,96,3072]{3,2,1,0:T(8,128)(2,1)}, bf16[2,2,96,3072]{3,2,1,0:T(8,128)(2,1)}, u32[]{:S(2)}, u32[]{:S(2)}) collective-permute-start(bf16[2,2,96,3072]{3,2,1,0:T(8,128)(2,1)} %dynamic-slice_bitcast_fusion.1), channel_id=1, source_target_pairs={{0,4},{4,0},{8,12},{12,8},{16,20},{20,16},{24,28},{28,24},{1,5},{5... | collective-permute-start | bytes 7077896 | tf_op jit(solution)/shard_map/ppermute | solution.py:90
  1092.6 108.1 %collective-permute-start.22 = (bf16[2,2,256,1536]{3,2,1,0:T(8,128)(2,1)S(1)}, bf16[2,2,256,1536]{3,2,1,0:T(8,128)(2,1)S(1)}, u32[]{:S(2)}, u32[]{:S(2)}) collective-permute-start(bf16[2,2,256,1536]{3,2,1,0:T(8,128)(2,1)S(1)} %dynamic-slice_bitcast_fusion), channel_id=1, source_target_pairs={{0,4},{4,0},{8,12},{12,8},{16,20},{20,16},{24,28},{28,24},{1,5},{5... | collective-permute-start | bytes 9437192 | tf_op jit(solution)/shard_map/ppermute | solution.py:90
  1093.6 107.1 %slice-start.5 = ((s8[6291456]{0:T(1024)(128)(4,1)}), s8[4194304]{0:T(1024)(128)(4,1)S(1)}, s32[]{:S(2)}) async-start(s8[6291456]{0:T(1024)(128)(4,1)} %bitcast.265), calls=%async_computation.9 | async-start | bytes 8388608
  1093.6 107.1 %slice-start.6 = ((s8[6291456]{0:T(1024)(128)(4,1)}), s8[2097152]{0:T(1024)(128)(4,1)S(1)}, s32[]{:S(2)}) async-start(s8[6291456]{0:T(1024)(128)(4,1)} %bitcast.265), calls=%async_computation.10 | async-start | bytes 4194304
  1138.2 150.6 %collective-permute-start.15 = (bf16[2,96,3072]{2,1,0:T(8,128)(2,1)}, bf16[2,96,3072]{2,1,0:T(8,128)(2,1)}, u32[]{:S(2)}, u32[]{:S(2)}) collective-permute-start(bf16[2,96,3072]{2,1,0:T(8,128)(2,1)} %dynamic-slice_bitcast_fusion.6), channel_id=1, source_target_pairs={{0,16},{4,20},{8,24},{12,28},{16,0},{20,4},{24,8},{28,12},{1,17},{... | collective-permute-start | bytes 3538952 | tf_op jit(solution)/shard_map/ppermute | solution.py:90
  1201.6 85.8 %copy-start.107 = (bf16[8,1,64]{2,1,0:T(2,128)(2,1)S(1)}, bf16[8,1,64]{2,1,0:T(2,128)(2,1)}, u32[]{:S(2)}) copy-start(bf16[8,1,64]{2,1,0:T(2,128)(2,1)} %constant_dynamic-slice_fusion.12) | copy-start | bytes 3076
  1201.6 85.8 %copy-start.113 = (f32[8]{0:T(128)S(1)}, f32[8]{0:T(128)}, u32[]{:S(2)}) copy-start(f32[8]{0:T(128)} %convert_divide_fusion) | copy-start | bytes 100
  1202.9 91.4 %collective-permute-start.23 = (bf16[2,256,1536]{2,1,0:T(8,128)(2,1)}, bf16[2,256,1536]{2,1,0:T(8,128)(2,1)}, u32[]{:S(2)}, u32[]{:S(2)}) collective-permute-start(bf16[2,256,1536]{2,1,0:T(8,128)(2,1)} %dynamic-slice_bitcast_fusion.5), channel_id=1, source_target_pairs={{0,16},{4,20},{8,24},{12,28},{16,0},{20,4},{24,8},{28,12},{1,17},{... | collective-permute-start | bytes 4718600 | tf_op jit(solution)/shard_map/ppermute | solution.py:90
  1290.9 17.5 %collective-permute-start.16 = (bf16[96,3072]{1,0:T(8,128)(2,1)S(1)}, bf16[96,3072]{1,0:T(8,128)(2,1)S(1)}, u32[]{:S(2)}, u32[]{:S(2)}) collective-permute-start(bf16[96,3072]{1,0:T(8,128)(2,1)S(1)} %dynamic-slice_bitcast_fusion.12), channel_id=1, source_target_pairs={{0,8},{4,12},{8,0},{12,4},{16,24},{20,28},{24,16},{28,20},{1,9},{5... | collective-permute-start | bytes 1769480 | tf_op jit(solution)/shard_map/ppermute | solution.py:90
  1296.1 28.8 %collective-permute-start.24 = (bf16[256,1536]{1,0:T(8,128)(2,1)S(1)}, bf16[256,1536]{1,0:T(8,128)(2,1)S(1)}, u32[]{:S(2)}, u32[]{:S(2)}) collective-permute-start(bf16[256,1536]{1,0:T(8,128)(2,1)S(1)} %dynamic-slice_bitcast_fusion.10), channel_id=1, source_target_pairs={{0,8},{4,12},{8,0},{12,4},{16,24},{20,28},{24,16},{28,20},{1,9},{5... | collective-permute-start | bytes 2359304 | tf_op jit(solution)/shard_map/ppermute | solution.py:90
  (130 other events, 1491.6 us)
Sparse Core Ops, SparseCore 0:
  9.6 15.1 all-gather.5
  26.3 17.9 all-gather.7
  45.8 17.9 all-gather.9
  192.1 16.9 all-gather.11
